TPU v7x, 32 devices: a whole 2x2x4 slice. The times are simulated.
32 devices in a mesh: grid: 8 (over z, core), tp: 4 (over y, x).
Axes of the slice: x: 2, y: 2, z: 4, core: 2. Of those that a mesh axis runs over, the one named last changes fastest.
Arguments:
- latents: bfloat16 [3072, 3072], P('grid'), may hold values from -6 to 6
- input_weight: bfloat16 [3072, 1536], P('grid', 'tp'), as said below
- norm_gains: float32 [2, 128], replicated, as said below
- text_pairs: bfloat16 [256, 1024], P(None, 'tp'), may hold values from -6 to 6
- text_count: int32 [1], replicated, may hold values from 64 to 256
- output_weight: bfloat16 [512, 3072], P('tp', 'grid'), may hold values from -0.25 to 0.25
Outputs:
- block_output: bfloat16 [3072, 3072], P('grid', 'tp')
Inputs may be any that keep to these rules, and one draw needn't show every extreme that they name: `text_count`: number of valid text tokens; the remaining text slots are padding. `input_weight`: a projection scaled by its fan-in. `norm_gains`: positive gains.
All inputs are finite; a program needn't handle non-finite values.
Results may differ from a plain program's by a relative error of at most 0.015.
Values may be sent and summed in bfloat16 or wider, within the bound.
No kernel may reach another device: no remote copies, remote signals or barrier semaphores. Data moves between devices by JAX's collectives and lax.ppermute only.
A program may use at most 64 MiB of HBM per device.

v0:
```python
import functools

import jax
import jax.numpy as jnp
import numpy as np
from jax import lax
from jax.experimental import pallas as pl
from jax.experimental.pallas import tpu as pltpu
from jax.sharding import PartitionSpec as P


GRID_H = 4
LOG2E = float(np.log2(np.e))

epsilon = 1e-06


F32 = jnp.float32
BF16 = jnp.bfloat16
VMEM = pl.BlockSpec(memory_space=pltpu.VMEM)
SMEM = pl.BlockSpec(memory_space=pltpu.SMEM)
GRANT = pltpu.CompilerParams(vmem_limit_bytes=16 * 1024 * 1024)


def shape_of(shape, dtype):
    return jax.ShapeDtypeStruct(shape, dtype)


def cost(flops, bytes_accessed, transcendentals=0):
    return pl.CostEstimate(
        flops=int(flops), bytes_accessed=int(bytes_accessed), transcendentals=int(transcendentals)
    )


def root_norm(values, gain):
    return values * lax.rsqrt(jnp.mean(values * values, axis=-1, keepdims=True) + epsilon) * gain


def partial_body(slots, carried, latents_ref, partner_ref, *refs):
    chips = lax.axis_size("grid") // 2
    place = lax.axis_index("grid")
    chip, core = place // 2, lax.rem(place, 2)
    weights, refs = refs[: len(slots)], refs[len(slots) :]
    if carried:
        carried_mine, carried_other = refs[:2]
        refs = refs[2:]
    mine_ref, other_ref = refs
    depth = weights[0].shape[0]

    def products(weight_ref, owner):
        columns = pl.ds(pl.multiple_of((2 * owner + core) * depth, depth), depth)
        weight = weight_ref[...]
        return (
            jnp.dot(latents_ref[:, columns], weight, preferred_element_type=F32),
            jnp.dot(partner_ref[:, columns], weight, preferred_element_type=F32),
        )

    mine = other = None
    if carried:
        mine, other = carried_mine[...], carried_other[...]
    for weight_ref, (owner_of, here) in zip(weights, slots):
        if here is None:
            add_mine, add_other = products(weight_ref, owner_of(chip))
            mine = add_mine if mine is None else mine + add_mine
            other = add_other if other is None else other + add_other
    mine_ref[...], other_ref[...] = mine, other
    for weight_ref, (owner_of, here) in zip(weights, slots):
        if here is not None:

            @pl.when(here(chip, chips))
            def _():
                add_mine, add_other = products(weight_ref, owner_of(chip))
                mine_ref[...] += add_mine
                other_ref[...] += add_other


def partial_product(latents, partner_latents, weights, slots, carry):
    rows = latents.shape[0]
    depth, width = weights[0].shape
    count = len(weights)
    carry = list(carry)
    return pl.pallas_call(
        functools.partial(partial_body, tuple(slots), bool(carry)),
        out_shape=[shape_of((rows, width), F32)] * 2,
        in_specs=[VMEM] * (2 + count + len(carry)),
        out_specs=[VMEM] * 2,
        cost_estimate=cost(4 * rows * depth * width * count, 4 * rows * depth * count),
        compiler_params=GRANT,
        name="partial_product",
    )(latents, partner_latents, *weights, *carry)


def finish_body(head_size, has_partner, *refs):
    total = refs[0][...]
    if has_partner:
        total = total + refs[1][...]
        refs = refs[1:]
    gains = refs[1][...]
    query_ref, pair_ref = refs[2:]
    query_ref[...] = root_norm(total[:, :head_size], gains[0:1]).astype(BF16)
    keys = root_norm(total[:, head_size : 2 * head_size], gains[1:2])
    pair_ref[:, :head_size] = keys.astype(BF16)
    pair_ref[:, head_size:] = total[:, 2 * head_size :].astype(BF16)


def finish_projection(parts, norm_gains):
    rows, width = parts[0].shape
    head_size = norm_gains.shape[1]
    return pl.pallas_call(
        functools.partial(finish_body, head_size, len(parts) > 1),
        out_shape=[shape_of((rows, head_size), BF16), shape_of((rows, 2 * head_size), BF16)],
        in_specs=[VMEM] * (len(parts) + 1),
        out_specs=[VMEM] * 2,
        cost_estimate=cost(10 * rows * width, 10 * rows * width, 2 * rows),
        compiler_params=GRANT,
        name="finish_projection",
    )(*parts, norm_gains)


def project(latents, input_weight, norm_gains):
    devices = lax.axis_size("grid")
    chips = devices // 2
    if devices % 2 or chips != 4:
        weight = lax.all_gather(input_weight, "grid", axis=0, tiled=True)
        total = jnp.dot(latents, weight, preferred_element_type=F32)
        return finish_projection([total], norm_gains)
    every = range(devices)
    swap = [(at, at ^ 1) for at in every]
    across = [(at, at ^ chips) for at in every]
    up = [(at, at + 2) for at in every if at + 2 < devices]
    down = [(at, at - 2) for at in every if at >= 2]
    outward = [(at, at - 2) for at in (2, 3)] + [
        (at, at + 2) for at in (devices - 4, devices - 3)
    ]
    far = lax.ppermute(input_weight, "grid", across)
    below = lax.ppermute(input_weight, "grid", up)
    above = lax.ppermute(input_weight, "grid", down)
    partner_latents = lax.ppermute(latents, "grid", swap)
    relayed = lax.ppermute(far, "grid", outward)
    half = chips // 2
    carry = partial_product(
        latents,
        partner_latents,
        [input_weight, far],
        [(lambda chip: chip, None), (lambda chip: lax.rem(chip + half, chips), None)],
        (),
    )
    carry = partial_product(
        latents,
        partner_latents,
        [below, above],
        [
            (lambda chip: chip - 1, lambda chip, chips: chip > 0),
            (lambda chip: chip + 1, lambda chip, chips: chip < chips - 1),
        ],
        carry,
    )
    mine, other = partial_product(
        latents,
        partner_latents,
        [relayed],
        [(lambda chip: chips - 1 - chip, lambda chip, chips: (chip == 0) | (chip == chips - 1))],
        carry,
    )
    return finish_projection([mine, lax.ppermute(other, "grid", swap)], norm_gains)


def attend(state, query, keys, values, factor, live=None):
    scores = lax.dot_general(query, keys, (((1,), (1,)), ((), ())), preferred_element_type=F32)
    if live is not None:
        scores = jnp.where(live, scores, -jnp.inf)
    top = scores.max(-1, keepdims=True)
    if state is None:
        weights = jnp.exp2((scores - top) * factor)
        mixed = jnp.dot(weights.astype(BF16), values, preferred_element_type=F32)
        return top, weights.sum(-1, keepdims=True), mixed
    old_top, old_sum, old_mixed = state
    top = jnp.maximum(old_top, top)
    fade = jnp.exp2((old_top - top) * factor)
    weights = jnp.exp2((scores - top) * factor)
    mixed = jnp.dot(weights.astype(BF16), values, preferred_element_type=F32)
    return top, old_sum * fade + weights.sum(-1, keepdims=True), old_mixed * fade + mixed


def outer_height(height):
    return jnp.where(lax.rem(height, 2) == 0, height - 1, height + 1)


def attend_body(slots, with_text, carried, last, factor, *refs):
    place = lax.axis_index("grid")
    times = lax.axis_size("grid") // GRID_H
    time, height = place // GRID_H, lax.rem(place, GRID_H)
    beyond = outer_height(height)
    outer_ok = (beyond >= 0) & (beyond < GRID_H)
    query_ref, refs = refs[0], refs[1:]
    pair_refs, refs = refs[: len(slots)], refs[len(slots) :]
    head_size = query_ref.shape[1]
    query = query_ref[...]
    rows = query.shape[0]
    state = None
    if with_text:
        count_ref, text_ref, gains_ref = refs[:3]
        refs = refs[3:]
    if carried:
        state = refs[0][:, 0:1], refs[1][:, 0:1], refs[2][...]
        refs = refs[3:]
    scratch = refs[-3:]
    outs = refs[:-3]
    if with_text:
        text_keys = root_norm(text_ref[:, :head_size].astype(F32), gains_ref[1:2]).astype(BF16)
        live = lax.broadcasted_iota(jnp.int32, (rows, text_ref.shape[0]), 1) < count_ref[0]
        state = attend(state, query, text_keys, text_ref[:, head_size:], factor, live)
    gates = []
    for by, outer in slots:
        gate = None
        if by is not None:
            gate = (time - by >= 0) & (time - by < times)
        if outer:
            gate = outer_ok if gate is None else gate & outer_ok
        gates.append(gate)
    for pair_ref, gate in zip(pair_refs, gates):
        if gate is None:
            pair = pair_ref[...]
            state = attend(state, query, pair[:, :head_size], pair[:, head_size:], factor)
    for pair_ref, gate in zip(pair_refs, gates):
        if gate is not None:
            scratch[0][...], scratch[1][...], scratch[2][...] = state

            @pl.when(gate)
            def _():
                pair = pair_ref[...]
                before = scratch[0][...], scratch[1][...], scratch[2][...]
                after = attend(before, query, pair[:, :head_size], pair[:, head_size:], factor)
                scratch[0][...], scratch[1][...], scratch[2][...] = after

            state = scratch[0][...], scratch[1][...], scratch[2][...]
    top, total, mixed = state
    if last:
        outs[0][...] = (mixed / total).astype(BF16)
    else:
        outs[0][...] = jnp.broadcast_to(top, outs[0].shape)
        outs[1][...] = jnp.broadcast_to(total, outs[1].shape)
        outs[2][...] = mixed


def attention_step(query, pairs, slots, text=(), carry=(), last=False):
    rows, head_size = query.shape
    factor = head_size ** (-0.5) * LOG2E
    text, carry = list(text), list(carry)
    plane = shape_of((rows, head_size), F32)
    columns = sum(pair.shape[0] for pair in pairs)
    return pl.pallas_call(
        functools.partial(attend_body, tuple(slots), bool(text), bool(carry), last, factor),
        out_shape=shape_of((rows, head_size), BF16) if last else [plane] * 3,
        in_specs=[VMEM] * (1 + len(pairs))
        + ([SMEM, VMEM, VMEM] if text else [])
        + [VMEM] * len(carry),
        out_specs=VMEM if last else [VMEM] * 3,
        scratch_shapes=[
            pltpu.VMEM((rows, 1), F32),
            pltpu.VMEM((rows, 1), F32),
            pltpu.VMEM((rows, head_size), F32),
        ],
        cost_estimate=cost(4 * rows * columns * head_size, 4 * columns * head_size, rows * columns),
        compiler_params=GRANT,
        name="attention_step",
    )(query, *pairs, *text, *carry)


def attention_rows(query, pair, text_pairs, norm_gains, text_count):
    devices = lax.axis_size("grid")
    times = devices // GRID_H
    swap = [(at, at ^ 1) for at in range(devices)]
    outer = []
    for at in range(devices):
        row = at % GRID_H
        beyond = row - 1 if row % 2 == 0 else row + 1
        if 0 <= beyond < GRID_H:
            outer.append((at, at - row + beyond))

    def later(pairs, by):
        return [(at, to + by * GRID_H) for at, to in pairs if 0 <= to + by * GRID_H < devices]

    same = [(at, at) for at in range(devices)]
    if times == 2:
        half = devices // 2
        plans = [(None, [(at, at ^ half) for at in range(devices)], [(at, to ^ half) for at, to in outer])]
    elif times > 2:
        plans = [(by, later(same, by), later(outer, by)) for by in (1, -1)]
    else:
        plans = []
    far = [lax.ppermute(pair, "grid", along) for _, along, _ in plans]
    partner = lax.ppermute(pair, "grid", swap)
    near_outer = lax.ppermute(pair, "grid", outer)
    far_outer = [lax.ppermute(pair, "grid", over) for _, _, over in plans]
    text = (text_count, text_pairs, norm_gains)
    carry = attention_step(query, [pair], [(None, False)], text=text)
    carry = attention_step(
        query, [partner, near_outer], [(None, False), (None, True)], carry=carry, last=not plans
    )
    for at, (by, _, _) in enumerate(plans):
        carry = attention_step(
            query, [far[at], far_outer[at]], [(by, False), (by, True)], carry=carry
        )
        carry = attention_step(
            query,
            [lax.ppermute(far[at], "grid", swap)],
            [(by, False)],
            carry=carry,
            last=at == len(plans) - 1,
        )
    return carry


def output_body(groups, *refs):
    attention, refs = refs[:groups], refs[groups:]
    mine_ref, other_ref, out_ref, held, joined = refs
    place, group = lax.axis_index("grid"), lax.axis_index("tp")
    chip, core = place // 2, lax.rem(place, 2)
    depth, width = mine_ref.shape[0] // groups, mine_ref.shape[1]
    for at in range(groups):
        held[at] = attention[at][...]
    for turn in range(groups):
        source = lax.rem(chip + groups - turn, groups)
        joined[:, turn * depth : (turn + 1) * depth] = held[group ^ source]
    rows = joined[...]
    mine = jnp.dot(rows, mine_ref[...], preferred_element_type=F32).astype(BF16)
    other = jnp.dot(rows, other_ref[...], preferred_element_type=F32).astype(BF16)

    @pl.when(core == 0)
    def _():
        out_ref[:, :width] = mine
        out_ref[:, width:] = other

    @pl.when(core != 0)
    def _():
        out_ref[:, :width] = other
        out_ref[:, width:] = mine


def output_product(attention, mine, other):
    groups = len(attention)
    rows, depth = attention[0].shape
    width = mine.shape[1]
    return pl.pallas_call(
        functools.partial(output_body, groups),
        out_shape=shape_of((rows, 2 * width), BF16),
        in_specs=[VMEM] * (groups + 2),
        out_specs=VMEM,
        scratch_shapes=[
            pltpu.VMEM((groups, rows, depth), BF16),
            pltpu.VMEM((rows, groups * depth), BF16),
        ],
        cost_estimate=cost(
            4 * rows * depth * groups * width, 4 * depth * groups * width + 4 * rows * width
        ),
        compiler_params=GRANT,
        name="output_product",
    )(*attention, mine, other)


def direct_output(devices, groups):
    return devices == 2 * groups and groups == 4


def send_output_weight(output_weight):
    groups = lax.axis_size("tp")

    def flat(chip, core, group):
        return (2 * chip + core) * groups + group

    pieces = []
    for turn in range(groups):
        pairs = [
            (flat(chip, core, group), flat((group + turn) % groups, core, chip))
            for chip in range(groups)
            for core in range(2)
            for group in range(groups)
        ]
        pieces.append(lax.ppermute(output_weight, ("grid", "tp"), pairs))
    return pieces


def local(latents, input_weight, norm_gains, text_pairs, text_count, output_weight):
    devices, groups = lax.axis_size("grid"), lax.axis_size("tp")
    direct = direct_output(devices, groups)
    if direct:
        pieces = send_output_weight(output_weight)
    query, pair = project(latents, input_weight, norm_gains)
    attention = attention_rows(query, pair, text_pairs, norm_gains, text_count)
    if not direct:
        weight = lax.all_gather(output_weight, "grid", axis=1, tiled=True)
        term = jnp.dot(attention, weight, preferred_element_type=F32)
        return lax.psum_scatter(term.astype(BF16), "tp", scatter_dimension=1, tiled=True)
    mine = jnp.concatenate(pieces, axis=0)
    other = lax.ppermute(mine, "grid", [(at, at ^ 1) for at in range(devices)])
    gathered = [attention] + [
        lax.ppermute(attention, "tp", [(at, at ^ by) for at in range(groups)])
        for by in range(1, groups)
    ]
    return output_product(gathered, mine, other)


def solution(mesh):
    placed = (P("grid", None), P("grid", "tp"), P(), P(None, "tp"), P(), P("tp", "grid"))
    return jax.shard_map(
        local, mesh=mesh, in_specs=placed, out_specs=P("grid", "tp"), check_vma=False
    )
```

profile of v0, /device:TPU:1, one launch (start us, length us, event | category | flops | bytes accessed | tf_op | source)
XLA Modules:
  0.0 73.0 jit_solution(17594072925867792841)
XLA Ops:
  0.0 3.8 %collective-permute-start.1 = (bf16[384,384]{1,0:T(8,128)(2,1)}, bf16[384,384]{1,0:T(8,128)(2,1)S(1)}, u32[]{:S(2)}, u32[]{:S(2)}) collective-permute-start(bf16[384,384]{1,0:T(8,128)(2,1)} %refs_0_.1), channel_id=1, source_target_pairs={{0,16},{4,20},{8,24},{12,28},{16,0},{20,4},{24,8},{28,12},{1,17},{... | collective-permute-start | bytes 884744 | tf_op jit(solution)/shard_map/ppermute | solution.py:135
  3.8 3.2 %collective-permute-start.3 = (bf16[384,384]{1,0:T(8,128)(2,1)}, bf16[384,384]{1,0:T(8,128)(2,1)S(1)}, u32[]{:S(2)}, u32[]{:S(2)}) collective-permute-start(bf16[384,384]{1,0:T(8,128)(2,1)} %refs_0_.1), channel_id=1, source_target_pairs={{0,8},{4,12},{8,16},{12,20},{16,24},{20,28},{1,9},{5,13},{9,17},{1... | collective-permute-start | bytes 884744 | tf_op jit(solution)/shard_map/ppermute | solution.py:136
  7.0 1.3 %collective-permute-start.4 = (bf16[384,384]{1,0:T(8,128)(2,1)}, bf16[384,384]{1,0:T(8,128)(2,1)S(1)}, u32[]{:S(2)}, u32[]{:S(2)}) collective-permute-start(bf16[384,384]{1,0:T(8,128)(2,1)} %refs_0_.1), channel_id=1, source_target_pairs={{8,0},{12,4},{16,8},{20,12},{24,16},{28,20},{9,1},{13,5},{17,9},{2... | collective-permute-start | bytes 884744 | tf_op jit(solution)/shard_map/ppermute | solution.py:137
  8.3 9.4 %collective-permute-done.1.refs_1_ = bf16[384,384]{1,0:T(8,128)(2,1)S(1)} collective-permute-done((bf16[384,384]{1,0:T(8,128)(2,1)}, bf16[384,384]{1,0:T(8,128)(2,1)S(1)}, u32[]{:S(2)}, u32[]{:S(2)}) %collective-permute-start.1) | collective-permute-done | bytes 294944 | tf_op jit(solution)/shard_map/ppermute | solution.py:135
  17.8 1.3 %collective-permute-start.2 = (bf16[384,384]{1,0:T(8,128)(2,1)S(1)}, bf16[384,384]{1,0:T(8,128)(2,1)S(1)}, u32[]{:S(2)}, u32[]{:S(2)}) collective-permute-start(bf16[384,384]{1,0:T(8,128)(2,1)S(1)} %collective-permute-done.1.refs_1_), channel_id=1, source_target_pairs={{8,0},{12,4},{16,24},{20,28},{9,1},{13,5},{17,25},{21,29},{10,2},{... | collective-permute-start | bytes 884744 | tf_op jit(solution)/shard_map/ppermute | solution.py:139
  19.1 1.7 %copy-done = bf16[384,3072]{1,0:T(8,128)(2,1)S(1)} copy-done((bf16[384,3072]{1,0:T(8,128)(2,1)S(1)}, bf16[384,3072]{1,0:T(8,128)(2,1)}, u32[]{:S(2)}) %copy-start) | copy-done | bytes 2359320
  23.2 5.6 %collective-permute-done.2.refs_0_ = bf16[384,384]{1,0:T(8,128)(2,1)S(1)} collective-permute-done((bf16[384,384]{1,0:T(8,128)(2,1)S(1)}, bf16[384,384]{1,0:T(8,128)(2,1)S(1)}, u32[]{:S(2)}, u32[]{:S(2)}) %collective-permute-start.2) | collective-permute-done | bytes 294944 | tf_op jit(solution)/shard_map/ppermute | solution.py:139
  29.5 1.2 %collective-permute-start.5 = (f32[384,384]{1,0:T(8,128)S(1)}, f32[384,384]{1,0:T(8,128)S(1)}, u32[]{:S(2)}, u32[]{:S(2)}) collective-permute-start(f32[384,384]{1,0:T(8,128)S(1)} %get-tuple-element.27), channel_id=1, source_target_pairs={{0,4},{4,0},{8,12},{12,8},{16,20},{20,16},{24,28},{28,24},{1,5},{5... | collective-permute-start | bytes 1769480 | tf_op jit(solution)/shard_map/ppermute | solution.py:165
  31.4 3.7 %collective-permute-start.15 = (bf16[128,384]{1,0:T(8,128)(2,1)S(1)}, bf16[128,384]{1,0:T(8,128)(2,1)S(1)}, u32[]{:S(2)}, u32[]{:S(2)}) collective-permute-start(bf16[128,384]{1,0:T(8,128)(2,1)S(1)} %copy-done.4), channel_id=1, source_target_pairs={{0,8},{1,16},{2,24},{3,0},{4,12},{5,20},{6,28},{7,4},{8,9},{9,17},... | collective-permute-start | bytes 294920 | tf_op jit(solution)/shard_map/ppermute | solution.py:380
  36.1 3.2 %collective-permute-start.17 = (bf16[128,384]{1,0:T(8,128)(2,1)S(1)}, bf16[128,384]{1,0:T(8,128)(2,1)S(1)}, u32[]{:S(2)}, u32[]{:S(2)}) collective-permute-start(bf16[128,384]{1,0:T(8,128)(2,1)S(1)} %copy-done.4), channel_id=1, source_target_pairs={{0,24},{1,0},{2,8},{3,16},{4,28},{5,4},{6,12},{7,20},{8,25},{9,1},... | collective-permute-start | bytes 294920 | tf_op jit(solution)/shard_map/ppermute | solution.py:380
  39.3 3.2 %collective-permute-done.15 = bf16[128,384]{1,0:T(8,128)(2,1)S(1)} collective-permute-done((bf16[128,384]{1,0:T(8,128)(2,1)S(1)}, bf16[128,384]{1,0:T(8,128)(2,1)S(1)}, u32[]{:S(2)}, u32[]{:S(2)}) %collective-permute-start.15) | collective-permute-done | bytes 98336 | tf_op jit(solution)/shard_map/ppermute | solution.py:380
  42.5 1.3 %collective-permute-done.16 = bf16[128,384]{1,0:T(8,128)(2,1)S(1)} collective-permute-done((bf16[128,384]{1,0:T(8,128)(2,1)S(1)}, bf16[128,384]{1,0:T(8,128)(2,1)S(1)}, u32[]{:S(2)}, u32[]{:S(2)}) %collective-permute-start.16) | collective-permute-done | bytes 98336 | tf_op jit(solution)/shard_map/ppermute | solution.py:380
  44.6 1.4 %collective-permute-start.18 = (bf16[512,384]{1,0:T(8,128)(2,1)S(1)}, bf16[512,384]{1,0:T(8,128)(2,1)S(1)}, u32[]{:S(2)}, u32[]{:S(2)}) collective-permute-start(bf16[512,384]{1,0:T(8,128)(2,1)S(1)} %constant_dynamic-update-slice_fusion.refs_4_), channel_id=1, source_target_pairs={{0,4},{4,0},{8,12},{12,8},{16,20},{20,16},{24,28},{28,24},{1,5},{5... | collective-permute-start | bytes 1179656 | tf_op jit(solution)/shard_map/ppermute | solution.py:396
  46.0 4.1 %collective-permute-start.10 = (bf16[384,256]{1,0:T(8,128)(2,1)S(1)}, bf16[384,256]{1,0:T(8,128)(2,1)S(1)}, u32[]{:S(2)}, u32[]{:S(2)}) collective-permute-start(bf16[384,256]{1,0:T(8,128)(2,1)S(1)} %get-tuple-element.29.refs_1_), channel_id=1, source_target_pairs={{4,8},{8,4},{20,24},{24,20},{5,9},{9,5},{21,25},{25,21},{6,10},{10... | collective-permute-start | bytes 589832 | tf_op jit(solution)/shard_map/ppermute | solution.py:294
  50.2 2.9 %collective-permute-start.8 = (bf16[384,256]{1,0:T(8,128)(2,1)S(1)}, bf16[384,256]{1,0:T(8,128)(2,1)S(1)}, u32[]{:S(2)}, u32[]{:S(2)}) collective-permute-start(bf16[384,256]{1,0:T(8,128)(2,1)S(1)} %get-tuple-element.29.refs_1_), channel_id=1, source_target_pairs={{4,24},{8,20},{20,8},{24,4},{5,25},{9,21},{21,9},{25,5},{6,26},{10... | collective-permute-start | bytes 589832 | tf_op jit(solution)/shard_map/ppermute | solution.py:295
  53.2 2.5 %collective-permute-done.6.refs_1_ = bf16[384,256]{1,0:T(8,128)(2,1)S(1)} collective-permute-done((bf16[384,256]{1,0:T(8,128)(2,1)S(1)}, bf16[384,256]{1,0:T(8,128)(2,1)S(1)}, u32[]{:S(2)}, u32[]{:S(2)}) %collective-permute-start.6) | collective-permute-done | bytes 196640 | tf_op jit(solution)/shard_map/ppermute | solution.py:292
  57.9 1.8 %collective-permute-done.10.refs_2_ = bf16[384,256]{1,0:T(8,128)(2,1)S(1)} collective-permute-done((bf16[384,256]{1,0:T(8,128)(2,1)S(1)}, bf16[384,256]{1,0:T(8,128)(2,1)S(1)}, u32[]{:S(2)}, u32[]{:S(2)}) %collective-permute-start.10) | collective-permute-done | bytes 196640 | tf_op jit(solution)/shard_map/ppermute | solution.py:294
  59.7 1.8 %attention_step.5 = (f32[384,128]{1,0:T(8,128)S(1)}, f32[384,128]{1,0:T(8,128)S(1)}, f32[384,128]{1,0:T(8,128)S(1)}) custom-call(bf16[384,128]{1,0:T(8,128)(2,1)S(1)} %get-tuple-element.28.refs_0_, bf16[384,256]{1,0:T(8,128)(2,1)S(1)} %collective-permute-done.9.refs_1_, bf16[384,256]{1,0:T(8,128)(2,1)S(1)} %collective-permute-done.10.refs_2_, ...), custom_call_target="tpu_custom_call" | custom-call | flops 150994944 | bytes 393216 | tf_op jit(solution)/shard_map/attention_step/pallas_call | solution.py:252
  61.5 1.8 %attention_step.6 = (f32[384,128]{1,0:T(8,128)S(1)}, f32[384,128]{1,0:T(8,128)S(1)}, f32[384,128]{1,0:T(8,128)S(1)}) custom-call(bf16[384,128]{1,0:T(8,128)(2,1)S(1)} %get-tuple-element.28.refs_0_, bf16[384,256]{1,0:T(8,128)(2,1)S(1)} %collective-permute-done.6.refs_1_, bf16[384,256]{1,0:T(8,128)(2,1)S(1)} %collective-permute-done.8.refs_2_, ...), custom_call_target="tpu_custom_call" | custom-call | flops 150994944 | bytes 393216 | tf_op jit(solution)/shard_map/attention_step/pallas_call | solution.py:252
  64.3 1.6 %collective-permute-start.11 = (bf16[384,128]{1,0:T(8,128)(2,1)S(1)}, bf16[384,128]{1,0:T(8,128)(2,1)S(1)}, u32[]{:S(2)}, u32[]{:S(2)}) collective-permute-start(bf16[384,128]{1,0:T(8,128)(2,1)S(1)} %attention_step.7.refs_0_), channel_id=1, source_target_pairs={{0,1},{1,0},{2,3},{3,2},{4,5},{5,4},{6,7},{7,6},{8,9},{9,8},{10,11... | collective-permute-start | bytes 294920 | tf_op jit(solution)/shard_map/ppermute | solution.py:398
  65.8 1.3 %collective-permute-start.12 = (bf16[384,128]{1,0:T(8,128)(2,1)S(1)}, bf16[384,128]{1,0:T(8,128)(2,1)S(1)}, u32[]{:S(2)}, u32[]{:S(2)}) collective-permute-start(bf16[384,128]{1,0:T(8,128)(2,1)S(1)} %attention_step.7.refs_0_), channel_id=1, source_target_pairs={{0,2},{1,3},{2,0},{3,1},{4,6},{5,7},{6,4},{7,5},{8,10},{9,11},{10,... | collective-permute-start | bytes 294920 | tf_op jit(solution)/shard_map/ppermute | solution.py:398
  68.6 1.7 %collective-permute-done.12.refs_2_ = bf16[384,128]{1,0:T(8,128)(2,1)S(1)} collective-permute-done((bf16[384,128]{1,0:T(8,128)(2,1)S(1)}, bf16[384,128]{1,0:T(8,128)(2,1)S(1)}, u32[]{:S(2)}, u32[]{:S(2)}) %collective-permute-start.12) | collective-permute-done | bytes 98336 | tf_op jit(solution)/shard_map/ppermute | solution.py:398
  70.3 1.2 %collective-permute-done.13.refs_3_ = bf16[384,128]{1,0:T(8,128)(2,1)S(1)} collective-permute-done((bf16[384,128]{1,0:T(8,128)(2,1)S(1)}, bf16[384,128]{1,0:T(8,128)(2,1)S(1)}, u32[]{:S(2)}, u32[]{:S(2)}) %collective-permute-start.13) | collective-permute-done | bytes 98336 | tf_op jit(solution)/shard_map/ppermute | solution.py:398
  71.5 1.5 %output_product.1 = bf16[384,768]{1,0:T(8,128)(2,1)} custom-call(bf16[384,128]{1,0:T(8,128)(2,1)S(1)} %attention_step.7.refs_0_, bf16[384,128]{1,0:T(8,128)(2,1)S(1)} %collective-permute-done.11.refs_1_, bf16[384,128]{1,0:T(8,128)(2,1)S(1)} %collective-permute-done.12.refs_2_, bf16[384,128]{1,0:T(8,128)(2,1)S(1)} %collective-permute-done.13.refs_3_, ...), custom_call_target="tpu_custom_call" | custom-call | flops 301989888 | bytes 1376256 | tf_op jit(solution)/shard_map/output_product/pallas_call | solution.py:345
  (37 shorter events, 9.6 us)
Async XLA Ops:
  0.0 19.1 %collective-permute-start = (bf16[384,3072]{1,0:T(8,128)(2,1)}, bf16[384,3072]{1,0:T(8,128)(2,1)S(1)}, u32[]{:S(2)}, u32[]{:S(2)}) collective-permute-start(bf16[384,3072]{1,0:T(8,128)(2,1)} %latents_ref.5), channel_id=1, source_target_pairs={{0,4},{4,0},{8,12},{12,8},{16,20},{20,16},{24,28},{28,24},{1,5},{5... | collective-permute-start | bytes 7077896 | tf_op jit(solution)/shard_map/ppermute | solution.py:138
  0.0 17.7 %collective-permute-start.1 = (bf16[384,384]{1,0:T(8,128)(2,1)}, bf16[384,384]{1,0:T(8,128)(2,1)S(1)}, u32[]{:S(2)}, u32[]{:S(2)}) collective-permute-start(bf16[384,384]{1,0:T(8,128)(2,1)} %refs_0_.1), channel_id=1, source_target_pairs={{0,16},{4,20},{8,24},{12,28},{16,0},{20,4},{24,8},{28,12},{1,17},{... | collective-permute-start | bytes 884744 | tf_op jit(solution)/shard_map/ppermute | solution.py:135
  3.8 18.8 %collective-permute-start.3 = (bf16[384,384]{1,0:T(8,128)(2,1)}, bf16[384,384]{1,0:T(8,128)(2,1)S(1)}, u32[]{:S(2)}, u32[]{:S(2)}) collective-permute-start(bf16[384,384]{1,0:T(8,128)(2,1)} %refs_0_.1), channel_id=1, source_target_pairs={{0,8},{4,12},{8,16},{12,20},{16,24},{20,28},{1,9},{5,13},{9,17},{1... | collective-permute-start | bytes 884744 | tf_op jit(solution)/shard_map/ppermute | solution.py:136
  7.0 15.6 %collective-permute-start.4 = (bf16[384,384]{1,0:T(8,128)(2,1)}, bf16[384,384]{1,0:T(8,128)(2,1)S(1)}, u32[]{:S(2)}, u32[]{:S(2)}) collective-permute-start(bf16[384,384]{1,0:T(8,128)(2,1)} %refs_0_.1), channel_id=1, source_target_pairs={{8,0},{12,4},{16,8},{20,12},{24,16},{28,20},{9,1},{13,5},{17,9},{2... | collective-permute-start | bytes 884744 | tf_op jit(solution)/shard_map/ppermute | solution.py:137
  17.8 11.1 %collective-permute-start.2 = (bf16[384,384]{1,0:T(8,128)(2,1)S(1)}, bf16[384,384]{1,0:T(8,128)(2,1)S(1)}, u32[]{:S(2)}, u32[]{:S(2)}) collective-permute-start(bf16[384,384]{1,0:T(8,128)(2,1)S(1)} %collective-permute-done.1.refs_1_), channel_id=1, source_target_pairs={{8,0},{12,4},{16,24},{20,28},{9,1},{13,5},{17,25},{21,29},{10,2},{... | collective-permute-start | bytes 884744 | tf_op jit(solution)/shard_map/ppermute | solution.py:139
  19.1 1.7 %copy-start = (bf16[384,3072]{1,0:T(8,128)(2,1)S(1)}, bf16[384,3072]{1,0:T(8,128)(2,1)}, u32[]{:S(2)}) copy-start(bf16[384,3072]{1,0:T(8,128)(2,1)} %latents_ref.5) | copy-start | bytes 7077892
  20.7 1.0 %copy-start.1 = (bf16[384,384]{1,0:T(8,128)(2,1)S(1)}, bf16[384,384]{1,0:T(8,128)(2,1)}, u32[]{:S(2)}) copy-start(bf16[384,384]{1,0:T(8,128)(2,1)} %refs_0_.1) | copy-start | bytes 884740
  28.9 1.8 %copy-start.4 = (bf16[128,384]{1,0:T(8,128)(2,1)S(1)}, bf16[128,384]{1,0:T(8,128)(2,1)}, u32[]{:S(2)}) copy-start(bf16[128,384]{1,0:T(8,128)(2,1)} %param.11) | copy-start | bytes 294916
  28.9 15.0 %copy-start.3 = (f32[2,128]{1,0:T(2,128)S(1)}, f32[2,128]{1,0:T(2,128)}, u32[]{:S(2)}) copy-start(f32[2,128]{1,0:T(2,128)} %refs_4_.1) | copy-start | bytes 3076
  28.9 28.1 %copy-start.2 = (bf16[256,256]{1,0:T(8,128)(2,1)S(1)}, bf16[256,256]{1,0:T(8,128)(2,1)}, u32[]{:S(2)}) copy-start(bf16[256,256]{1,0:T(8,128)(2,1)} %refs_3_.1) | copy-start | bytes 393220
  29.5 14.4 %collective-permute-start.5 = (f32[384,384]{1,0:T(8,128)S(1)}, f32[384,384]{1,0:T(8,128)S(1)}, u32[]{:S(2)}, u32[]{:S(2)}) collective-permute-start(f32[384,384]{1,0:T(8,128)S(1)} %get-tuple-element.27), channel_id=1, source_target_pairs={{0,4},{4,0},{8,12},{12,8},{16,20},{20,16},{24,28},{28,24},{1,5},{5... | collective-permute-start | bytes 1769480 | tf_op jit(solution)/shard_map/ppermute | solution.py:165
  30.7 8.6 %collective-permute-start.14 = (bf16[128,384]{1,0:T(8,128)(2,1)S(1)}, bf16[128,384]{1,0:T(8,128)(2,1)S(1)}, u32[]{:S(2)}, u32[]{:S(2)}) collective-permute-start(bf16[128,384]{1,0:T(8,128)(2,1)S(1)} %copy-done.4), channel_id=1, source_target_pairs={{0,0},{1,8},{2,16},{3,24},{4,4},{5,12},{6,20},{7,28},{8,1},{9,9},{... | collective-permute-start | bytes 294920 | tf_op jit(solution)/shard_map/ppermute | solution.py:380
  31.4 11.2 %collective-permute-start.15 = (bf16[128,384]{1,0:T(8,128)(2,1)S(1)}, bf16[128,384]{1,0:T(8,128)(2,1)S(1)}, u32[]{:S(2)}, u32[]{:S(2)}) collective-permute-start(bf16[128,384]{1,0:T(8,128)(2,1)S(1)} %copy-done.4), channel_id=1, source_target_pairs={{0,8},{1,16},{2,24},{3,0},{4,12},{5,20},{6,28},{7,4},{8,9},{9,17},... | collective-permute-start | bytes 294920 | tf_op jit(solution)/shard_map/ppermute | solution.py:380
  35.1 8.7 %collective-permute-start.16 = (bf16[128,384]{1,0:T(8,128)(2,1)S(1)}, bf16[128,384]{1,0:T(8,128)(2,1)S(1)}, u32[]{:S(2)}, u32[]{:S(2)}) collective-permute-start(bf16[128,384]{1,0:T(8,128)(2,1)S(1)} %copy-done.4), channel_id=1, source_target_pairs={{0,16},{1,24},{2,0},{3,8},{4,20},{5,28},{6,4},{7,12},{8,17},{9,25}... | collective-permute-start | bytes 294920 | tf_op jit(solution)/shard_map/ppermute | solution.py:380
  36.1 8.5 %collective-permute-start.17 = (bf16[128,384]{1,0:T(8,128)(2,1)S(1)}, bf16[128,384]{1,0:T(8,128)(2,1)S(1)}, u32[]{:S(2)}, u32[]{:S(2)}) collective-permute-start(bf16[128,384]{1,0:T(8,128)(2,1)S(1)} %copy-done.4), channel_id=1, source_target_pairs={{0,24},{1,0},{2,8},{3,16},{4,28},{5,4},{6,12},{7,20},{8,25},{9,1},... | collective-permute-start | bytes 294920 | tf_op jit(solution)/shard_map/ppermute | solution.py:380
  44.0 11.7 %collective-permute-start.6 = (bf16[384,256]{1,0:T(8,128)(2,1)S(1)}, bf16[384,256]{1,0:T(8,128)(2,1)S(1)}, u32[]{:S(2)}, u32[]{:S(2)}) collective-permute-start(bf16[384,256]{1,0:T(8,128)(2,1)S(1)} %get-tuple-element.29.refs_1_), channel_id=1, source_target_pairs={{0,16},{4,20},{8,24},{12,28},{16,0},{20,4},{24,8},{28,12},{1,17},{... | collective-permute-start | bytes 589832 | tf_op jit(solution)/shard_map/ppermute | solution.py:292
  44.6 23.7 %collective-permute-start.18 = (bf16[512,384]{1,0:T(8,128)(2,1)S(1)}, bf16[512,384]{1,0:T(8,128)(2,1)S(1)}, u32[]{:S(2)}, u32[]{:S(2)}) collective-permute-start(bf16[512,384]{1,0:T(8,128)(2,1)S(1)} %constant_dynamic-update-slice_fusion.refs_4_), channel_id=1, source_target_pairs={{0,4},{4,0},{8,12},{12,8},{16,20},{20,16},{24,28},{28,24},{1,5},{5... | collective-permute-start | bytes 1179656 | tf_op jit(solution)/shard_map/ppermute | solution.py:396
  46.0 13.7 %collective-permute-start.10 = (bf16[384,256]{1,0:T(8,128)(2,1)S(1)}, bf16[384,256]{1,0:T(8,128)(2,1)S(1)}, u32[]{:S(2)}, u32[]{:S(2)}) collective-permute-start(bf16[384,256]{1,0:T(8,128)(2,1)S(1)} %get-tuple-element.29.refs_1_), channel_id=1, source_target_pairs={{4,8},{8,4},{20,24},{24,20},{5,9},{9,5},{21,25},{25,21},{6,10},{10... | collective-permute-start | bytes 589832 | tf_op jit(solution)/shard_map/ppermute | solution.py:294
  50.2 9.5 %collective-permute-start.9 = (bf16[384,256]{1,0:T(8,128)(2,1)S(1)}, bf16[384,256]{1,0:T(8,128)(2,1)S(1)}, u32[]{:S(2)}, u32[]{:S(2)}) collective-permute-start(bf16[384,256]{1,0:T(8,128)(2,1)S(1)} %get-tuple-element.29.refs_1_), channel_id=1, source_target_pairs={{0,4},{4,0},{8,12},{12,8},{16,20},{20,16},{24,28},{28,24},{1,5},{5... | collective-permute-start | bytes 589832 | tf_op jit(solution)/shard_map/ppermute | solution.py:293
  50.2 11.2 %collective-permute-start.8 = (bf16[384,256]{1,0:T(8,128)(2,1)S(1)}, bf16[384,256]{1,0:T(8,128)(2,1)S(1)}, u32[]{:S(2)}, u32[]{:S(2)}) collective-permute-start(bf16[384,256]{1,0:T(8,128)(2,1)S(1)} %get-tuple-element.29.refs_1_), channel_id=1, source_target_pairs={{4,24},{8,20},{20,8},{24,4},{5,25},{9,21},{21,9},{25,5},{6,26},{10... | collective-permute-start | bytes 589832 | tf_op jit(solution)/shard_map/ppermute | solution.py:295
  55.7 7.5 %collective-permute-start.7 = (bf16[384,256]{1,0:T(8,128)(2,1)S(1)}, bf16[384,256]{1,0:T(8,128)(2,1)S(1)}, u32[]{:S(2)}, u32[]{:S(2)}) collective-permute-start(bf16[384,256]{1,0:T(8,128)(2,1)S(1)} %collective-permute-done.6.refs_1_), channel_id=1, source_target_pairs={{0,4},{4,0},{8,12},{12,8},{16,20},{20,16},{24,28},{28,24},{1,5},{5... | collective-permute-start | bytes 589832 | tf_op jit(solution)/shard_map/ppermute | solution.py:307
  64.3 4.4 %collective-permute-start.11 = (bf16[384,128]{1,0:T(8,128)(2,1)S(1)}, bf16[384,128]{1,0:T(8,128)(2,1)S(1)}, u32[]{:S(2)}, u32[]{:S(2)}) collective-permute-start(bf16[384,128]{1,0:T(8,128)(2,1)S(1)} %attention_step.7.refs_0_), channel_id=1, source_target_pairs={{0,1},{1,0},{2,3},{3,2},{4,5},{5,4},{6,7},{7,6},{8,9},{9,8},{10,11... | collective-permute-start | bytes 294920 | tf_op jit(solution)/shard_map/ppermute | solution.py:398
  65.8 4.4 %collective-permute-start.12 = (bf16[384,128]{1,0:T(8,128)(2,1)S(1)}, bf16[384,128]{1,0:T(8,128)(2,1)S(1)}, u32[]{:S(2)}, u32[]{:S(2)}) collective-permute-start(bf16[384,128]{1,0:T(8,128)(2,1)S(1)} %attention_step.7.refs_0_), channel_id=1, source_target_pairs={{0,2},{1,3},{2,0},{3,1},{4,6},{5,7},{6,4},{7,5},{8,10},{9,11},{10,... | collective-permute-start | bytes 294920 | tf_op jit(solution)/shard_map/ppermute | solution.py:398
  67.2 4.4 %collective-permute-start.13 = (bf16[384,128]{1,0:T(8,128)(2,1)S(1)}, bf16[384,128]{1,0:T(8,128)(2,1)S(1)}, u32[]{:S(2)}, u32[]{:S(2)}) collective-permute-start(bf16[384,128]{1,0:T(8,128)(2,1)S(1)} %attention_step.7.refs_0_), channel_id=1, source_target_pairs={{0,3},{1,2},{2,1},{3,0},{4,7},{5,6},{6,5},{7,4},{8,11},{9,10},{10,... | collective-permute-start | bytes 294920 | tf_op jit(solution)/shard_map/ppermute | solution.py:398
where the time goes:
time: 73.3 us; the launch traced here: 73 us
  starting transfers between devices  33.1 us (45%)
  waiting for transfers between devices  27.2 us (37%)
  Pallas kernels  9.21 us (13%)
  local copies, waits for them, and re-layouts  2.69 us (4%)
  between operations  0.84 us (1%)
    ppermute x1, waiting for transfers between devices, project(): far = lax.ppermute(input_weight, 'grid', across)  9.44 us
    ppermute x4, starting transfers between devices, send_output_weight(): pieces.append(lax.ppermute(output_weight, ('grid', 'tp'), pairs))  8.59 us
    ppermute x1, waiting for transfers between devices, project(): relayed = lax.ppermute(far, 'grid', outward)  5.64 us
    pallas_call x4, Pallas kernels, attention_step(): pl.pallas_call(functools.partial(attend_body, tuple(slots), bool(text), b...  5.46 us
    ppermute x4, waiting for transfers between devices, send_output_weight(): pieces.append(lax.ppermute(output_weight, ('grid', 'tp'), pairs))  4.48 us
    ppermute x1, starting transfers between devices, attention_rows(): near_outer = lax.ppermute(pair, 'grid', outer)  4.11 us
    ppermute x3, starting transfers between devices, local(): lax.ppermute(attention, 'tp', [(at, at ^ by) for at in range(groups)])  4.01 us
    ppermute x1, starting transfers between devices, project(): far = lax.ppermute(input_weight, 'grid', across)  3.78 us
  transfers between devices with their start and end apart: 19, of which 9 were waited for; matrix products, arithmetic and copies ran while one was open for 0% of the time, Pallas kernels for 10%

commit v1 on v0

--- a/solution.py
+++ b/solution.py
@@ -90,40 +90,41 @@
     )(latents, partner_latents, *weights, *carry)
 
 
-def finish_body(head_size, has_partner, *refs):
-    total = refs[0][...]
-    if has_partner:
-        total = total + refs[1][...]
-        refs = refs[1:]
-    gains = refs[1][...]
-    query_ref, pair_ref = refs[2:]
-    query_ref[...] = root_norm(total[:, :head_size], gains[0:1]).astype(BF16)
-    keys = root_norm(total[:, head_size : 2 * head_size], gains[1:2])
+def keys_body(head_size, mine_ref, other_ref, gains_ref, pair_ref):
+    total = mine_ref[...] + other_ref[...]
+    keys = root_norm(total[:, :head_size], gains_ref[1:2])
     pair_ref[:, :head_size] = keys.astype(BF16)
-    pair_ref[:, head_size:] = total[:, 2 * head_size :].astype(BF16)
-
-
-def finish_projection(parts, norm_gains):
-    rows, width = parts[0].shape
-    head_size = norm_gains.shape[1]
+    pair_ref[:, head_size:] = total[:, head_size:].astype(BF16)
+
+
+def query_body(mine_ref, other_ref, gains_ref, query_ref):
+    query_ref[...] = root_norm(mine_ref[...] + other_ref[...], gains_ref[0:1]).astype(BF16)
+
+
+def finish(body, mine, other, norm_gains):
+    rows, width = mine.shape
     return pl.pallas_call(
-        functools.partial(finish_body, head_size, len(parts) > 1),
-        out_shape=[shape_of((rows, head_size), BF16), shape_of((rows, 2 * head_size), BF16)],
-        in_specs=[VMEM] * (len(parts) + 1),
-        out_specs=[VMEM] * 2,
-        cost_estimate=cost(10 * rows * width, 10 * rows * width, 2 * rows),
+        body,
+        out_shape=shape_of((rows, width), BF16),
+        in_specs=[VMEM] * 3,
+        out_specs=VMEM,
+        cost_estimate=cost(10 * rows * width, 10 * rows * width, rows),
         compiler_params=GRANT,
-        name="finish_projection",
-    )(*parts, norm_gains)
+    )(mine, other, norm_gains)
 
 
 def project(latents, input_weight, norm_gains):
     devices = lax.axis_size("grid")
     chips = devices // 2
+    head_size = norm_gains.shape[1]
+    finish_keys = functools.partial(keys_body, head_size)
     if devices % 2 or chips != 4:
         weight = lax.all_gather(input_weight, "grid", axis=0, tiled=True)
         total = jnp.dot(latents, weight, preferred_element_type=F32)
-        return finish_projection([total], norm_gains)
+        zero = jnp.zeros_like(total)
+        query = finish(query_body, total[:, :head_size], zero[:, :head_size], norm_gains)
+        pair = finish(finish_keys, total[:, head_size:], zero[:, head_size:], norm_gains)
+        return query, pair
     every = range(devices)
     swap = [(at, at ^ 1) for at in every]
     across = [(at, at ^ chips) for at in every]
@@ -132,16 +133,21 @@
     outward = [(at, at - 2) for at in (2, 3)] + [
         (at, at + 2) for at in (devices - 4, devices - 3)
     ]
-    far = lax.ppermute(input_weight, "grid", across)
-    below = lax.ppermute(input_weight, "grid", up)
-    above = lax.ppermute(input_weight, "grid", down)
+    half = chips // 2
+    pair_weight, query_weight = input_weight[:, head_size:], input_weight[:, :head_size]
+    far = lax.ppermute(pair_weight, "grid", across)
+    below = lax.ppermute(pair_weight, "grid", up)
+    above = lax.ppermute(pair_weight, "grid", down)
     partner_latents = lax.ppermute(latents, "grid", swap)
     relayed = lax.ppermute(far, "grid", outward)
-    half = chips // 2
+    query_shards = [query_weight] + [
+        lax.ppermute(query_weight, "grid", [(at, (at + 2 * turn) % devices) for at in every])
+        for turn in range(1, chips)
+    ]
     carry = partial_product(
         latents,
         partner_latents,
-        [input_weight, far],
+        [pair_weight, far],
         [(lambda chip: chip, None), (lambda chip: lax.rem(chip + half, chips), None)],
         (),
     )
@@ -162,7 +168,19 @@
         [(lambda chip: chips - 1 - chip, lambda chip, chips: (chip == 0) | (chip == chips - 1))],
         carry,
     )
-    return finish_projection([mine, lax.ppermute(other, "grid", swap)], norm_gains)
+    pair = finish(finish_keys, mine, lax.ppermute(other, "grid", swap), norm_gains)
+    mine, other = partial_product(
+        latents,
+        partner_latents,
+        query_shards,
+        [
+            (lambda chip, turn=turn: lax.rem(chip + chips - turn, chips), None)
+            for turn in range(chips)
+        ],
+        (),
+    )
+    query = finish(query_body, mine, lax.ppermute(other, "grid", swap), norm_gains)
+    return query, pair
 
 
 def attend(state, query, keys, values, factor, live=None):
@@ -289,23 +307,25 @@
         plans = [(by, later(same, by), later(outer, by)) for by in (1, -1)]
     else:
         plans = []
+
+    def filled(pairs):
+        sources, targets = {at for at, _ in pairs}, {to for _, to in pairs}
+        return pairs + [(at, at) for at in range(devices) if at not in sources and at not in targets]
+
     far = [lax.ppermute(pair, "grid", along) for _, along, _ in plans]
     partner = lax.ppermute(pair, "grid", swap)
-    near_outer = lax.ppermute(pair, "grid", outer)
-    far_outer = [lax.ppermute(pair, "grid", over) for _, _, over in plans]
+    near_outer = lax.ppermute(pair, "grid", filled(outer))
+    far_outer = [lax.ppermute(pair, "grid", filled(over)) for _, _, over in plans]
     text = (text_count, text_pairs, norm_gains)
-    carry = attention_step(query, [pair], [(None, False)], text=text)
-    carry = attention_step(
-        query, [partner, near_outer], [(None, False), (None, True)], carry=carry, last=not plans
-    )
+    carry = attention_step(query, [pair, partner], [(None, False), (None, False)], text=text)
+    carry = attention_step(query, [near_outer], [(None, True)], carry=carry, last=not plans)
     for at, (by, _, _) in enumerate(plans):
-        carry = attention_step(
-            query, [far[at], far_outer[at]], [(by, False), (by, True)], carry=carry
-        )
+        far_partner = lax.ppermute(far[at], "grid", swap)
+        carry = attention_step(query, [far[at]], [(by, False)], carry=carry)
         carry = attention_step(
             query,
-            [lax.ppermute(far[at], "grid", swap)],
-            [(by, False)],
+            [far_partner, far_outer[at]],
+            [(by, False), (by, True)],
             carry=carry,
             last=at == len(plans) - 1,
         )

time: 73.3 us -> 88.7 us (1.21)
  the two profiles are of different devices: /device:TPU:1 before, /device:TPU:10 now
where the time goes in v1:
time: 88.7 us; the launch traced here: 88.4 us
  starting transfers between devices  47.4 us (53%)
  waiting for transfers between devices  27.5 us (31%)
  Pallas kernels  8.96 us (10%)
  local copies, waits for them, and re-layouts  3.59 us (4%)
  between operations  0.95 us (1%)
    ppermute x4, waiting for transfers between devices, send_output_weight(): pieces.append(lax.ppermute(output_weight, ('grid', 'tp'), pairs))  17.5 us
    ppermute x4, starting transfers between devices, send_output_weight(): pieces.append(lax.ppermute(output_weight, ('grid', 'tp'), pairs))  13.4 us
    ppermute x3, starting transfers between devices, local(): lax.ppermute(attention, 'tp', [(at, at ^ by) for at in range(groups)])  6.76 us
    ppermute x3, starting transfers between devices, project(): lax.ppermute(query_weight, 'grid', [(at, (at + 2 * turn) % devices) for a...  6.28 us
    ppermute x3, waiting for transfers between devices, local(): lax.ppermute(attention, 'tp', [(at, at ^ by) for at in range(groups)])  5.51 us
    pallas_call x4, Pallas kernels, attention_step(): pl.pallas_call(functools.partial(attend_body, tuple(slots), bool(text), b...  5.01 us
    ppermute x1, starting transfers between devices, attention_rows(): near_outer = lax.ppermute(pair, 'grid', filled(outer))  4.06 us
    ppermute x1, starting transfers between devices, attention_rows(): lax.ppermute(pair, 'grid', filled(over))  3.99 us
  transfers between devices with their start and end apart: 23, of which 7 were waited for; matrix products, arithmetic and copies ran while one was open for 2% of the time, Pallas kernels for 8%

profile of v1, /device:TPU:10, one launch (start us, length us, event | category | flops | bytes accessed | tf_op | source)
XLA Modules:
  0.0 88.4 jit_solution(16911348770214567389)
XLA Ops:
  0.9 2.7 %collective-permute-start.5 = (bf16[384,256]{1,0:T(8,128)(2,1)S(1)}, bf16[384,256]{1,0:T(8,128)(2,1)S(1)}, u32[]{:S(2)}, u32[]{:S(2)}) collective-permute-start(bf16[384,256]{1,0:T(8,128)(2,1)S(1)} %slice.7.refs_0_), channel_id=1, source_target_pairs={{0,16},{4,20},{8,24},{12,28},{16,0},{20,4},{24,8},{28,12},{1,17},{... | collective-permute-start | bytes 589832 | tf_op jit(solution)/shard_map/ppermute | solution.py:138
  3.6 1.9 %collective-permute-start.7 = (bf16[384,256]{1,0:T(8,128)(2,1)S(1)}, bf16[384,256]{1,0:T(8,128)(2,1)S(1)}, u32[]{:S(2)}, u32[]{:S(2)}) collective-permute-start(bf16[384,256]{1,0:T(8,128)(2,1)S(1)} %slice.7.refs_0_), channel_id=1, source_target_pairs={{0,8},{4,12},{8,16},{12,20},{16,24},{20,28},{1,9},{5,13},{9,17},{1... | collective-permute-start | bytes 589832 | tf_op jit(solution)/shard_map/ppermute | solution.py:139
  5.5 3.9 %collective-permute-start.8 = (bf16[384,256]{1,0:T(8,128)(2,1)S(1)}, bf16[384,256]{1,0:T(8,128)(2,1)S(1)}, u32[]{:S(2)}, u32[]{:S(2)}) collective-permute-start(bf16[384,256]{1,0:T(8,128)(2,1)S(1)} %slice.7.refs_0_), channel_id=1, source_target_pairs={{8,0},{12,4},{16,8},{20,12},{24,16},{28,20},{9,1},{13,5},{17,9},{2... | collective-permute-start | bytes 589832 | tf_op jit(solution)/shard_map/ppermute | solution.py:140
  9.5 3.2 %collective-permute-done.5.refs_1_ = bf16[384,256]{1,0:T(8,128)(2,1)S(1)} collective-permute-done((bf16[384,256]{1,0:T(8,128)(2,1)S(1)}, bf16[384,256]{1,0:T(8,128)(2,1)S(1)}, u32[]{:S(2)}, u32[]{:S(2)}) %collective-permute-start.5) | collective-permute-done | bytes 196640 | tf_op jit(solution)/shard_map/ppermute | solution.py:138
  12.6 3.6 %collective-permute-start.6 = (bf16[384,256]{1,0:T(8,128)(2,1)S(1)}, bf16[384,256]{1,0:T(8,128)(2,1)S(1)}, u32[]{:S(2)}, u32[]{:S(2)}) collective-permute-start(bf16[384,256]{1,0:T(8,128)(2,1)S(1)} %collective-permute-done.5.refs_1_), channel_id=1, source_target_pairs={{8,0},{12,4},{16,24},{20,28},{9,1},{13,5},{17,25},{21,29},{10,2},{... | collective-permute-start | bytes 589832 | tf_op jit(solution)/shard_map/ppermute | solution.py:142
  16.3 1.6 %collective-permute-start.18 = (bf16[128,384]{1,0:T(8,128)(2,1)}, bf16[128,384]{1,0:T(8,128)(2,1)S(1)}, u32[]{:S(2)}, u32[]{:S(2)}) collective-permute-start(bf16[128,384]{1,0:T(8,128)(2,1)} %param.11), channel_id=1, source_target_pairs={{0,0},{1,8},{2,16},{3,24},{4,4},{5,12},{6,20},{7,28},{8,1},{9,9},{... | collective-permute-start | bytes 294920 | tf_op jit(solution)/shard_map/ppermute | solution.py:400
  17.8 1.7 %copy-done = bf16[384,3072]{1,0:T(8,128)(2,1)S(1)} copy-done((bf16[384,3072]{1,0:T(8,128)(2,1)S(1)}, bf16[384,3072]{1,0:T(8,128)(2,1)}, u32[]{:S(2)}) %copy-start) | copy-done | bytes 2359320
  21.9 3.3 %collective-permute-start.1 = (bf16[384,128]{1,0:T(8,128)(2,1)S(1)}, bf16[384,128]{1,0:T(8,128)(2,1)S(1)}, u32[]{:S(2)}, u32[]{:S(2)}) collective-permute-start(bf16[384,128]{1,0:T(8,128)(2,1)S(1)} %slice.6.refs_0_), channel_id=1, source_target_pairs={{0,8},{4,12},{8,16},{12,20},{16,24},{20,28},{24,0},{28,4},{1,9},{5... | collective-permute-start | bytes 294920 | tf_op jit(solution)/shard_map/ppermute | solution.py:144
  25.3 1.1 %collective-permute-start.2 = (bf16[384,128]{1,0:T(8,128)(2,1)S(1)}, bf16[384,128]{1,0:T(8,128)(2,1)S(1)}, u32[]{:S(2)}, u32[]{:S(2)}) collective-permute-start(bf16[384,128]{1,0:T(8,128)(2,1)S(1)} %slice.6.refs_0_), channel_id=1, source_target_pairs={{0,16},{4,20},{8,24},{12,28},{16,0},{20,4},{24,8},{28,12},{1,17},{... | collective-permute-start | bytes 294920 | tf_op jit(solution)/shard_map/ppermute | solution.py:144
  26.4 1.9 %collective-permute-start.3 = (bf16[384,128]{1,0:T(8,128)(2,1)S(1)}, bf16[384,128]{1,0:T(8,128)(2,1)S(1)}, u32[]{:S(2)}, u32[]{:S(2)}) collective-permute-start(bf16[384,128]{1,0:T(8,128)(2,1)S(1)} %slice.6.refs_0_), channel_id=1, source_target_pairs={{0,24},{4,28},{8,0},{12,4},{16,8},{20,12},{24,16},{28,20},{1,25},{... | collective-permute-start | bytes 294920 | tf_op jit(solution)/shard_map/ppermute | solution.py:144
  29.0 9.5 %collective-permute-done.19 = bf16[128,384]{1,0:T(8,128)(2,1)S(1)} collective-permute-done((bf16[128,384]{1,0:T(8,128)(2,1)S(1)}, bf16[128,384]{1,0:T(8,128)(2,1)S(1)}, u32[]{:S(2)}, u32[]{:S(2)}) %collective-permute-start.19) | collective-permute-done | bytes 98336 | tf_op jit(solution)/shard_map/ppermute | solution.py:400
  38.5 5.1 %collective-permute-start.20 = (bf16[128,384]{1,0:T(8,128)(2,1)S(1)}, bf16[128,384]{1,0:T(8,128)(2,1)S(1)}, u32[]{:S(2)}, u32[]{:S(2)}) collective-permute-start(bf16[128,384]{1,0:T(8,128)(2,1)S(1)} %copy-done.3), channel_id=1, source_target_pairs={{0,16},{1,24},{2,0},{3,8},{4,20},{5,28},{6,4},{7,12},{8,17},{9,25}... | collective-permute-start | bytes 294920 | tf_op jit(solution)/shard_map/ppermute | solution.py:400
  43.6 4.3 %collective-permute-done.20 = bf16[128,384]{1,0:T(8,128)(2,1)S(1)} collective-permute-done((bf16[128,384]{1,0:T(8,128)(2,1)S(1)}, bf16[128,384]{1,0:T(8,128)(2,1)S(1)}, u32[]{:S(2)}, u32[]{:S(2)}) %collective-permute-start.20) | collective-permute-done | bytes 98336 | tf_op jit(solution)/shard_map/ppermute | solution.py:400
  47.9 6.0 %collective-permute-start.21 = (bf16[128,384]{1,0:T(8,128)(2,1)S(1)}, bf16[128,384]{1,0:T(8,128)(2,1)S(1)}, u32[]{:S(2)}, u32[]{:S(2)}) collective-permute-start(bf16[128,384]{1,0:T(8,128)(2,1)S(1)} %copy-done.3), channel_id=1, source_target_pairs={{0,24},{1,0},{2,8},{3,16},{4,28},{5,4},{6,12},{7,20},{8,25},{9,1},... | collective-permute-start | bytes 294920 | tf_op jit(solution)/shard_map/ppermute | solution.py:400
  55.0 3.8 %collective-permute-done.21 = bf16[128,384]{1,0:T(8,128)(2,1)S(1)} collective-permute-done((bf16[128,384]{1,0:T(8,128)(2,1)S(1)}, bf16[128,384]{1,0:T(8,128)(2,1)S(1)}, u32[]{:S(2)}, u32[]{:S(2)}) %collective-permute-start.21) | collective-permute-done | bytes 98336 | tf_op jit(solution)/shard_map/ppermute | solution.py:400
  59.4 4.1 %collective-permute-start.13 = (bf16[384,256]{1,0:T(8,128)(2,1)S(1)}, bf16[384,256]{1,0:T(8,128)(2,1)S(1)}, u32[]{:S(2)}, u32[]{:S(2)}) collective-permute-start(bf16[384,256]{1,0:T(8,128)(2,1)S(1)} %shard_map.65.refs_1_), channel_id=1, source_target_pairs={{4,8},{8,4},{20,24},{24,20},{0,0},{12,12},{16,16},{28,28},{5,9},{9... | collective-permute-start | bytes 589832 | tf_op jit(solution)/shard_map/ppermute | solution.py:317
  63.5 4.0 %collective-permute-start.12 = (bf16[384,256]{1,0:T(8,128)(2,1)S(1)}, bf16[384,256]{1,0:T(8,128)(2,1)S(1)}, u32[]{:S(2)}, u32[]{:S(2)}) collective-permute-start(bf16[384,256]{1,0:T(8,128)(2,1)S(1)} %shard_map.65.refs_1_), channel_id=1, source_target_pairs={{4,24},{8,20},{20,8},{24,4},{0,0},{12,12},{16,16},{28,28},{5,25},{... | collective-permute-start | bytes 589832 | tf_op jit(solution)/shard_map/ppermute | solution.py:318
  68.4 1.2 %attention_step.4 = (f32[384,128]{1,0:T(8,128)S(1)}, f32[384,128]{1,0:T(8,128)S(1)}, f32[384,128]{1,0:T(8,128)S(1)}) custom-call(bf16[384,128]{1,0:T(8,128)(2,1)S(1)} %shard_map.64.refs_0_, bf16[384,256]{1,0:T(8,128)(2,1)S(1)} %shard_map.65.refs_1_, bf16[384,256]{1,0:T(8,128)(2,1)S(1)} %collective-permute-done.14.refs_2_, s32[1]{0:T(128)S(6)} %copy.10.refs_3_, ...), custom_call_target="tpu_custom_call" | custom-call | flops 150994944 | bytes 393216 | tf_op jit(solution)/shard_map/attention_step/pallas_call | solution.py:270
  71.7 1.2 %collective-permute-done.12.refs_2_ = bf16[384,256]{1,0:T(8,128)(2,1)S(1)} collective-permute-done((bf16[384,256]{1,0:T(8,128)(2,1)S(1)}, bf16[384,256]{1,0:T(8,128)(2,1)S(1)}, u32[]{:S(2)}, u32[]{:S(2)}) %collective-permute-start.12) | collective-permute-done | bytes 196640 | tf_op jit(solution)/shard_map/ppermute | solution.py:318
  72.9 1.7 %attention_step.7.refs_0_ = bf16[384,128]{1,0:T(8,128)(2,1)S(1)} custom-call(bf16[384,128]{1,0:T(8,128)(2,1)S(1)} %shard_map.64.refs_0_, bf16[384,256]{1,0:T(8,128)(2,1)S(1)} %collective-permute-done.11.refs_1_, bf16[384,256]{1,0:T(8,128)(2,1)S(1)} %collective-permute-done.12.refs_2_, f32[384,128]{1,0:T(8,128)S(1)} %get-tuple-element.36.refs_3_, ...), custom_call_target="tpu_custom_call" | custom-call | flops 150994944 | bytes 393216 | tf_op jit(solution)/shard_map/attention_step/pallas_call | solution.py:270
  74.7 6.7 %collective-permute-start.16 = (bf16[384,128]{1,0:T(8,128)(2,1)S(1)}, bf16[384,128]{1,0:T(8,128)(2,1)S(1)}, u32[]{:S(2)}, u32[]{:S(2)}) collective-permute-start(bf16[384,128]{1,0:T(8,128)(2,1)S(1)} %attention_step.7.refs_0_), channel_id=1, source_target_pairs={{0,2},{1,3},{2,0},{3,1},{4,6},{5,7},{6,4},{7,5},{8,10},{9,11},{10,... | collective-permute-start | bytes 294920 | tf_op jit(solution)/shard_map/ppermute | solution.py:418
  81.4 2.6 %collective-permute-done.16.refs_2_ = bf16[384,128]{1,0:T(8,128)(2,1)S(1)} collective-permute-done((bf16[384,128]{1,0:T(8,128)(2,1)S(1)}, bf16[384,128]{1,0:T(8,128)(2,1)S(1)}, u32[]{:S(2)}, u32[]{:S(2)}) %collective-permute-start.16) | collective-permute-done | bytes 98336 | tf_op jit(solution)/shard_map/ppermute | solution.py:418
  84.0 2.9 %collective-permute-done.17.refs_3_ = bf16[384,128]{1,0:T(8,128)(2,1)S(1)} collective-permute-done((bf16[384,128]{1,0:T(8,128)(2,1)S(1)}, bf16[384,128]{1,0:T(8,128)(2,1)S(1)}, u32[]{:S(2)}, u32[]{:S(2)}) %collective-permute-start.17) | collective-permute-done | bytes 98336 | tf_op jit(solution)/shard_map/ppermute | solution.py:418
  86.9 1.5 %output_product.1 = bf16[384,768]{1,0:T(8,128)(2,1)} custom-call(bf16[384,128]{1,0:T(8,128)(2,1)S(1)} %attention_step.7.refs_0_, bf16[384,128]{1,0:T(8,128)(2,1)S(1)} %collective-permute-done.15.refs_1_, bf16[384,128]{1,0:T(8,128)(2,1)S(1)} %collective-permute-done.16.refs_2_, bf16[384,128]{1,0:T(8,128)(2,1)S(1)} %collective-permute-done.17.refs_3_, ...), custom_call_target="tpu_custom_call" | custom-call | flops 301989888 | bytes 1376256 | tf_op jit(solution)/shard_map/output_product/pallas_call | solution.py:365
  (47 shorter events, 8.2 us)
Async XLA Ops:
  0.0 17.8 %collective-permute-start = (bf16[384,3072]{1,0:T(8,128)(2,1)}, bf16[384,3072]{1,0:T(8,128)(2,1)S(1)}, u32[]{:S(2)}, u32[]{:S(2)}) collective-permute-start(bf16[384,3072]{1,0:T(8,128)(2,1)} %latents_ref.7), channel_id=1, source_target_pairs={{0,4},{4,0},{8,12},{12,8},{16,20},{20,16},{24,28},{28,24},{1,5},{5... | collective-permute-start | bytes 7077896 | tf_op jit(solution)/shard_map/ppermute | solution.py:141
  0.9 11.7 %collective-permute-start.5 = (bf16[384,256]{1,0:T(8,128)(2,1)S(1)}, bf16[384,256]{1,0:T(8,128)(2,1)S(1)}, u32[]{:S(2)}, u32[]{:S(2)}) collective-permute-start(bf16[384,256]{1,0:T(8,128)(2,1)S(1)} %slice.7.refs_0_), channel_id=1, source_target_pairs={{0,16},{4,20},{8,24},{12,28},{16,0},{20,4},{24,8},{28,12},{1,17},{... | collective-permute-start | bytes 589832 | tf_op jit(solution)/shard_map/ppermute | solution.py:138
  3.6 16.5 %collective-permute-start.7 = (bf16[384,256]{1,0:T(8,128)(2,1)S(1)}, bf16[384,256]{1,0:T(8,128)(2,1)S(1)}, u32[]{:S(2)}, u32[]{:S(2)}) collective-permute-start(bf16[384,256]{1,0:T(8,128)(2,1)S(1)} %slice.7.refs_0_), channel_id=1, source_target_pairs={{0,8},{4,12},{8,16},{12,20},{16,24},{20,28},{1,9},{5,13},{9,17},{1... | collective-permute-start | bytes 589832 | tf_op jit(solution)/shard_map/ppermute | solution.py:139
  5.5 14.6 %collective-permute-start.8 = (bf16[384,256]{1,0:T(8,128)(2,1)S(1)}, bf16[384,256]{1,0:T(8,128)(2,1)S(1)}, u32[]{:S(2)}, u32[]{:S(2)}) collective-permute-start(bf16[384,256]{1,0:T(8,128)(2,1)S(1)} %slice.7.refs_0_), channel_id=1, source_target_pairs={{8,0},{12,4},{16,8},{20,12},{24,16},{28,20},{9,1},{13,5},{17,9},{2... | collective-permute-start | bytes 589832 | tf_op jit(solution)/shard_map/ppermute | solution.py:140
  12.6 8.3 %collective-permute-start.6 = (bf16[384,256]{1,0:T(8,128)(2,1)S(1)}, bf16[384,256]{1,0:T(8,128)(2,1)S(1)}, u32[]{:S(2)}, u32[]{:S(2)}) collective-permute-start(bf16[384,256]{1,0:T(8,128)(2,1)S(1)} %collective-permute-done.5.refs_1_), channel_id=1, source_target_pairs={{8,0},{12,4},{16,24},{20,28},{9,1},{13,5},{17,25},{21,29},{10,2},{... | collective-permute-start | bytes 589832 | tf_op jit(solution)/shard_map/ppermute | solution.py:142
  16.3 12.0 %collective-permute-start.18 = (bf16[128,384]{1,0:T(8,128)(2,1)}, bf16[128,384]{1,0:T(8,128)(2,1)S(1)}, u32[]{:S(2)}, u32[]{:S(2)}) collective-permute-start(bf16[128,384]{1,0:T(8,128)(2,1)} %param.11), channel_id=1, source_target_pairs={{0,0},{1,8},{2,16},{3,24},{4,4},{5,12},{6,20},{7,28},{8,1},{9,9},{... | collective-permute-start | bytes 294920 | tf_op jit(solution)/shard_map/ppermute | solution.py:400
  21.0 33.8 %collective-permute-start.9 = (f32[384,256]{1,0:T(8,128)S(1)}, f32[384,256]{1,0:T(8,128)S(1)}, u32[]{:S(2)}, u32[]{:S(2)}) collective-permute-start(f32[384,256]{1,0:T(8,128)S(1)} %get-tuple-element.29), channel_id=1, source_target_pairs={{0,4},{4,0},{8,12},{12,8},{16,20},{20,16},{24,28},{28,24},{1,5},{5... | collective-permute-start | bytes 1179656 | tf_op jit(solution)/shard_map/ppermute | solution.py:171
  21.9 31.9 %collective-permute-start.1 = (bf16[384,128]{1,0:T(8,128)(2,1)S(1)}, bf16[384,128]{1,0:T(8,128)(2,1)S(1)}, u32[]{:S(2)}, u32[]{:S(2)}) collective-permute-start(bf16[384,128]{1,0:T(8,128)(2,1)S(1)} %slice.6.refs_0_), channel_id=1, source_target_pairs={{0,8},{4,12},{8,16},{12,20},{16,24},{20,28},{24,0},{28,4},{1,9},{5... | collective-permute-start | bytes 294920 | tf_op jit(solution)/shard_map/ppermute | solution.py:144
  25.3 28.6 %collective-permute-start.2 = (bf16[384,128]{1,0:T(8,128)(2,1)S(1)}, bf16[384,128]{1,0:T(8,128)(2,1)S(1)}, u32[]{:S(2)}, u32[]{:S(2)}) collective-permute-start(bf16[384,128]{1,0:T(8,128)(2,1)S(1)} %slice.6.refs_0_), channel_id=1, source_target_pairs={{0,16},{4,20},{8,24},{12,28},{16,0},{20,4},{24,8},{28,12},{1,17},{... | collective-permute-start | bytes 294920 | tf_op jit(solution)/shard_map/ppermute | solution.py:144
  26.4 27.5 %collective-permute-start.3 = (bf16[384,128]{1,0:T(8,128)(2,1)S(1)}, bf16[384,128]{1,0:T(8,128)(2,1)S(1)}, u32[]{:S(2)}, u32[]{:S(2)}) collective-permute-start(bf16[384,128]{1,0:T(8,128)(2,1)S(1)} %slice.6.refs_0_), channel_id=1, source_target_pairs={{0,24},{4,28},{8,0},{12,4},{16,8},{20,12},{24,16},{28,20},{1,25},{... | collective-permute-start | bytes 294920 | tf_op jit(solution)/shard_map/ppermute | solution.py:144
  28.2 10.3 %collective-permute-start.19 = (bf16[128,384]{1,0:T(8,128)(2,1)S(1)}, bf16[128,384]{1,0:T(8,128)(2,1)S(1)}, u32[]{:S(2)}, u32[]{:S(2)}) collective-permute-start(bf16[128,384]{1,0:T(8,128)(2,1)S(1)} %copy-done.3), channel_id=1, source_target_pairs={{0,8},{1,16},{2,24},{3,0},{4,12},{5,20},{6,28},{7,4},{8,9},{9,17},... | collective-permute-start | bytes 294920 | tf_op jit(solution)/shard_map/ppermute | solution.py:400
  38.5 9.3 %collective-permute-start.20 = (bf16[128,384]{1,0:T(8,128)(2,1)S(1)}, bf16[128,384]{1,0:T(8,128)(2,1)S(1)}, u32[]{:S(2)}, u32[]{:S(2)}) collective-permute-start(bf16[128,384]{1,0:T(8,128)(2,1)S(1)} %copy-done.3), channel_id=1, source_target_pairs={{0,16},{1,24},{2,0},{3,8},{4,20},{5,28},{6,4},{7,12},{8,17},{9,25}... | collective-permute-start | bytes 294920 | tf_op jit(solution)/shard_map/ppermute | solution.py:400
  47.9 10.9 %collective-permute-start.21 = (bf16[128,384]{1,0:T(8,128)(2,1)S(1)}, bf16[128,384]{1,0:T(8,128)(2,1)S(1)}, u32[]{:S(2)}, u32[]{:S(2)}) collective-permute-start(bf16[128,384]{1,0:T(8,128)(2,1)S(1)} %copy-done.3), channel_id=1, source_target_pairs={{0,24},{1,0},{2,8},{3,16},{4,28},{5,4},{6,12},{7,20},{8,25},{9,1},... | collective-permute-start | bytes 294920 | tf_op jit(solution)/shard_map/ppermute | solution.py:400
  53.9 14.5 %copy-start.1 = (bf16[256,256]{1,0:T(8,128)(2,1)S(1)}, bf16[256,256]{1,0:T(8,128)(2,1)}, u32[]{:S(2)}) copy-start(bf16[256,256]{1,0:T(8,128)(2,1)} %refs_4_.1) | copy-start | bytes 393220
  54.7 8.8 %collective-permute-start.4 = (f32[384,128]{1,0:T(8,128)S(1)}, f32[384,128]{1,0:T(8,128)S(1)}, u32[]{:S(2)}, u32[]{:S(2)}) collective-permute-start(f32[384,128]{1,0:T(8,128)S(1)} %get-tuple-element.23), channel_id=1, source_target_pairs={{0,4},{4,0},{8,12},{12,8},{16,20},{20,16},{24,28},{28,24},{1,5},{5... | collective-permute-start | bytes 589832 | tf_op jit(solution)/shard_map/ppermute | solution.py:182
  55.0 12.5 %collective-permute-start.10 = (bf16[384,256]{1,0:T(8,128)(2,1)S(1)}, bf16[384,256]{1,0:T(8,128)(2,1)S(1)}, u32[]{:S(2)}, u32[]{:S(2)}) collective-permute-start(bf16[384,256]{1,0:T(8,128)(2,1)S(1)} %shard_map.65.refs_1_), channel_id=1, source_target_pairs={{0,16},{4,20},{8,24},{12,28},{16,0},{20,4},{24,8},{28,12},{1,17},{... | collective-permute-start | bytes 589832 | tf_op jit(solution)/shard_map/ppermute | solution.py:315
  58.8 22.6 %collective-permute-start.22 = (bf16[512,384]{1,0:T(8,128)(2,1)S(1)}, bf16[512,384]{1,0:T(8,128)(2,1)S(1)}, u32[]{:S(2)}, u32[]{:S(2)}) collective-permute-start(bf16[512,384]{1,0:T(8,128)(2,1)S(1)} %constant_dynamic-update-slice_fusion.refs_4_), channel_id=1, source_target_pairs={{0,4},{4,0},{8,12},{12,8},{16,20},{20,16},{24,28},{28,24},{1,5},{5... | collective-permute-start | bytes 1179656 | tf_op jit(solution)/shard_map/ppermute | solution.py:416
  58.9 9.5 %collective-permute-start.14 = (bf16[384,256]{1,0:T(8,128)(2,1)S(1)}, bf16[384,256]{1,0:T(8,128)(2,1)S(1)}, u32[]{:S(2)}, u32[]{:S(2)}) collective-permute-start(bf16[384,256]{1,0:T(8,128)(2,1)S(1)} %shard_map.65.refs_1_), channel_id=1, source_target_pairs={{0,4},{4,0},{8,12},{12,8},{16,20},{20,16},{24,28},{28,24},{1,5},{5... | collective-permute-start | bytes 589832 | tf_op jit(solution)/shard_map/ppermute | solution.py:316
  59.4 10.2 %collective-permute-start.13 = (bf16[384,256]{1,0:T(8,128)(2,1)S(1)}, bf16[384,256]{1,0:T(8,128)(2,1)S(1)}, u32[]{:S(2)}, u32[]{:S(2)}) collective-permute-start(bf16[384,256]{1,0:T(8,128)(2,1)S(1)} %shard_map.65.refs_1_), channel_id=1, source_target_pairs={{4,8},{8,4},{20,24},{24,20},{0,0},{12,12},{16,16},{28,28},{5,9},{9... | collective-permute-start | bytes 589832 | tf_op jit(solution)/shard_map/ppermute | solution.py:317
  63.5 9.4 %collective-permute-start.12 = (bf16[384,256]{1,0:T(8,128)(2,1)S(1)}, bf16[384,256]{1,0:T(8,128)(2,1)S(1)}, u32[]{:S(2)}, u32[]{:S(2)}) collective-permute-start(bf16[384,256]{1,0:T(8,128)(2,1)S(1)} %shard_map.65.refs_1_), channel_id=1, source_target_pairs={{4,24},{8,20},{20,8},{24,4},{0,0},{12,12},{16,16},{28,28},{5,25},{... | collective-permute-start | bytes 589832 | tf_op jit(solution)/shard_map/ppermute | solution.py:318
  67.5 5.4 %collective-permute-start.11 = (bf16[384,256]{1,0:T(8,128)(2,1)S(1)}, bf16[384,256]{1,0:T(8,128)(2,1)S(1)}, u32[]{:S(2)}, u32[]{:S(2)}) collective-permute-start(bf16[384,256]{1,0:T(8,128)(2,1)S(1)} %collective-permute-done.10.refs_1_), channel_id=1, source_target_pairs={{0,4},{4,0},{8,12},{12,8},{16,20},{20,16},{24,28},{28,24},{1,5},{5... | collective-permute-start | bytes 589832 | tf_op jit(solution)/shard_map/ppermute | solution.py:323
  74.6 6.8 %collective-permute-start.15 = (bf16[384,128]{1,0:T(8,128)(2,1)S(1)}, bf16[384,128]{1,0:T(8,128)(2,1)S(1)}, u32[]{:S(2)}, u32[]{:S(2)}) collective-permute-start(bf16[384,128]{1,0:T(8,128)(2,1)S(1)} %attention_step.7.refs_0_), channel_id=1, source_target_pairs={{0,1},{1,0},{2,3},{3,2},{4,5},{5,4},{6,7},{7,6},{8,9},{9,8},{10,11... | collective-permute-start | bytes 294920 | tf_op jit(solution)/shard_map/ppermute | solution.py:418
  74.7 9.3 %collective-permute-start.16 = (bf16[384,128]{1,0:T(8,128)(2,1)S(1)}, bf16[384,128]{1,0:T(8,128)(2,1)S(1)}, u32[]{:S(2)}, u32[]{:S(2)}) collective-permute-start(bf16[384,128]{1,0:T(8,128)(2,1)S(1)} %attention_step.7.refs_0_), channel_id=1, source_target_pairs={{0,2},{1,3},{2,0},{3,1},{4,6},{5,7},{6,4},{7,5},{8,10},{9,11},{10,... | collective-permute-start | bytes 294920 | tf_op jit(solution)/shard_map/ppermute | solution.py:418
  81.4 5.5 %collective-permute-start.17 = (bf16[384,128]{1,0:T(8,128)(2,1)S(1)}, bf16[384,128]{1,0:T(8,128)(2,1)S(1)}, u32[]{:S(2)}, u32[]{:S(2)}) collective-permute-start(bf16[384,128]{1,0:T(8,128)(2,1)S(1)} %attention_step.7.refs_0_), channel_id=1, source_target_pairs={{0,3},{1,2},{2,1},{3,0},{4,7},{5,6},{6,5},{7,4},{8,11},{9,10},{10,... | collective-permute-start | bytes 294920 | tf_op jit(solution)/shard_map/ppermute | solution.py:418
  (3 other events, 10.0 us)

commit v2 on v1

--- a/solution.py
+++ b/solution.py
@@ -111,6 +111,11 @@
         cost_estimate=cost(10 * rows * width, 10 * rows * width, rows),
         compiler_params=GRANT,
     )(mine, other, norm_gains)
+
+
+def filled(pairs, devices):
+    sources, targets = {at for at, _ in pairs}, {to for _, to in pairs}
+    return pairs + [(at, at) for at in range(devices) if at not in sources | targets]
 
 
 def project(latents, input_weight, norm_gains):
@@ -183,21 +188,34 @@
     return query, pair
 
 
-def attend(state, query, keys, values, factor, live=None):
-    scores = lax.dot_general(query, keys, (((1,), (1,)), ((), ())), preferred_element_type=F32)
-    if live is not None:
-        scores = jnp.where(live, scores, -jnp.inf)
-    top = scores.max(-1, keepdims=True)
-    if state is None:
-        weights = jnp.exp2((scores - top) * factor)
-        mixed = jnp.dot(weights.astype(BF16), values, preferred_element_type=F32)
-        return top, weights.sum(-1, keepdims=True), mixed
-    old_top, old_sum, old_mixed = state
-    top = jnp.maximum(old_top, top)
-    fade = jnp.exp2((old_top - top) * factor)
-    weights = jnp.exp2((scores - top) * factor)
-    mixed = jnp.dot(weights.astype(BF16), values, preferred_element_type=F32)
-    return top, old_sum * fade + weights.sum(-1, keepdims=True), old_mixed * fade + mixed
+def attend(state, query, tiles, factor):
+    rows, head_size = query.shape
+    scores = []
+    for keys, _, live in tiles:
+        score = lax.dot_general(query, keys, (((1,), (1,)), ((), ())), preferred_element_type=F32)
+        for at in range(0, keys.shape[0], head_size):
+            part = score[:, at : at + head_size]
+            if live is not None:
+                part = jnp.where(live[:, at : at + head_size], part, -jnp.inf)
+            scores.append(part)
+    top = functools.reduce(jnp.maximum, scores).max(-1, keepdims=True)
+    top = jnp.broadcast_to(top, (rows, head_size)) * factor
+    if state is not None:
+        top = jnp.maximum(state[0], top)
+    mixed = None
+    at = 0
+    for keys, values, _ in tiles:
+        count = keys.shape[0] // head_size
+        weights = [jnp.exp2(part * factor - top).astype(BF16) for part in scores[at : at + count]]
+        at += count
+        wide = jnp.concatenate([values, jnp.ones_like(values)], axis=1)
+        add = jnp.dot(jnp.concatenate(weights, axis=1), wide, preferred_element_type=F32)
+        mixed = add if mixed is None else mixed + add
+    total, mixed = mixed[:, head_size:], mixed[:, :head_size]
+    if state is not None:
+        fade = jnp.exp2(state[0] - top)
+        total, mixed = state[1] * fade + total, state[2] * fade + mixed
+    return top, total, mixed
 
 
 def outer_height(height):
@@ -213,52 +231,69 @@
     query_ref, refs = refs[0], refs[1:]
     pair_refs, refs = refs[: len(slots)], refs[len(slots) :]
     head_size = query_ref.shape[1]
-    query = query_ref[...]
-    rows = query.shape[0]
-    state = None
+    rows = query_ref.shape[0]
     if with_text:
         count_ref, text_ref, gains_ref = refs[:3]
         refs = refs[3:]
     if carried:
-        state = refs[0][:, 0:1], refs[1][:, 0:1], refs[2][...]
-        refs = refs[3:]
-    scratch = refs[-3:]
-    outs = refs[:-3]
-    if with_text:
-        text_keys = root_norm(text_ref[:, :head_size].astype(F32), gains_ref[1:2]).astype(BF16)
-        live = lax.broadcasted_iota(jnp.int32, (rows, text_ref.shape[0]), 1) < count_ref[0]
-        state = attend(state, query, text_keys, text_ref[:, head_size:], factor, live)
-    gates = []
-    for by, outer in slots:
-        gate = None
-        if by is not None:
-            gate = (time - by >= 0) & (time - by < times)
-        if outer:
-            gate = outer_ok if gate is None else gate & outer_ok
-        gates.append(gate)
-    for pair_ref, gate in zip(pair_refs, gates):
-        if gate is None:
-            pair = pair_ref[...]
-            state = attend(state, query, pair[:, :head_size], pair[:, head_size:], factor)
-    for pair_ref, gate in zip(pair_refs, gates):
-        if gate is not None:
-            scratch[0][...], scratch[1][...], scratch[2][...] = state
-
-            @pl.when(gate)
-            def _():
-                pair = pair_ref[...]
-                before = scratch[0][...], scratch[1][...], scratch[2][...]
-                after = attend(before, query, pair[:, :head_size], pair[:, head_size:], factor)
-                scratch[0][...], scratch[1][...], scratch[2][...] = after
-
-            state = scratch[0][...], scratch[1][...], scratch[2][...]
-    top, total, mixed = state
+        carry, refs = refs[:3], refs[3:]
+    held = refs[1:] if last else refs
+    out_ref = refs[0]
+
+    def before():
+        return tuple(ref[...] for ref in carry) if carried else None
+
+    def tiles_of(which):
+        return [
+            (pair_refs[at][:, :head_size], pair_refs[at][:, head_size:], None) for at in which
+        ]
+
+    def keep(state):
+        held[0][...], held[1][...], held[2][...] = state
+
+    def finish(state):
+        if last:
+            out_ref[...] = (state[2] / state[1]).astype(BF16)
+        else:
+            keep(state)
+
+    always = [at for at, (by, outer) in enumerate(slots) if by is None and not outer]
+    sometimes = [at for at in range(len(slots)) if at not in always]
+    if all(slots[at][0] is None for at in sometimes):
+        if with_text:
+            text_keys = root_norm(text_ref[:, :head_size].astype(F32), gains_ref[1:2]).astype(BF16)
+            live = lax.broadcasted_iota(jnp.int32, (rows, text_ref.shape[0]), 1) < count_ref[0]
+            extra = [(text_keys, text_ref[:, head_size:], live)]
+        else:
+            extra = []
+        if not sometimes:
+            finish(attend(before(), query_ref[...], extra + tiles_of(always), factor))
+            return
+
+        @pl.when(outer_ok)
+        def _():
+            both = extra + tiles_of(always + sometimes)
+            finish(attend(before(), query_ref[...], both, factor))
+
+        @pl.when(jnp.logical_not(outer_ok))
+        def _():
+            some = extra + tiles_of(always)
+            finish(attend(before(), query_ref[...], some, factor) if some else before())
+
+        return
+    keep(before())
+    for at in range(len(slots)):
+        by, outer = slots[at]
+        gate = (time - by >= 0) & (time - by < times)
+        gate = gate & outer_ok if outer else gate
+
+        @pl.when(gate)
+        def _():
+            state = held[0][...], held[1][...], held[2][...]
+            keep(attend(state, query_ref[...], tiles_of([at]), factor))
+
     if last:
-        outs[0][...] = (mixed / total).astype(BF16)
-    else:
-        outs[0][...] = jnp.broadcast_to(top, outs[0].shape)
-        outs[1][...] = jnp.broadcast_to(total, outs[1].shape)
-        outs[2][...] = mixed
+        finish((held[0][...], held[1][...], held[2][...]))
 
 
 def attention_step(query, pairs, slots, text=(), carry=(), last=False):
@@ -274,11 +309,7 @@
         + ([SMEM, VMEM, VMEM] if text else [])
         + [VMEM] * len(carry),
         out_specs=VMEM if last else [VMEM] * 3,
-        scratch_shapes=[
-            pltpu.VMEM((rows, 1), F32),
-            pltpu.VMEM((rows, 1), F32),
-            pltpu.VMEM((rows, head_size), F32),
-        ],
+        scratch_shapes=[pltpu.VMEM((rows, head_size), F32)] * 3 if last else [],
         cost_estimate=cost(4 * rows * columns * head_size, 4 * columns * head_size, rows * columns),
         compiler_params=GRANT,
         name="attention_step",
@@ -307,21 +338,20 @@
         plans = [(by, later(same, by), later(outer, by)) for by in (1, -1)]
     else:
         plans = []
-
-    def filled(pairs):
-        sources, targets = {at for at, _ in pairs}, {to for _, to in pairs}
-        return pairs + [(at, at) for at in range(devices) if at not in sources and at not in targets]
-
     far = [lax.ppermute(pair, "grid", along) for _, along, _ in plans]
     partner = lax.ppermute(pair, "grid", swap)
-    near_outer = lax.ppermute(pair, "grid", filled(outer))
-    far_outer = [lax.ppermute(pair, "grid", filled(over)) for _, _, over in plans]
+    near_outer = lax.ppermute(pair, "grid", filled(outer, devices))
+    far_outer = [lax.ppermute(pair, "grid", filled(over, devices)) for _, _, over in plans]
     text = (text_count, text_pairs, norm_gains)
     carry = attention_step(query, [pair, partner], [(None, False), (None, False)], text=text)
-    carry = attention_step(query, [near_outer], [(None, True)], carry=carry, last=not plans)
+    if not plans:
+        return attention_step(query, [near_outer], [(None, True)], carry=carry, last=True)
     for at, (by, _, _) in enumerate(plans):
         far_partner = lax.ppermute(far[at], "grid", swap)
-        carry = attention_step(query, [far[at]], [(by, False)], carry=carry)
+        near, near_slots = ([near_outer], [(None, True)]) if by is None else ([], [])
+        if by is not None and at == 0:
+            carry = attention_step(query, [near_outer], [(None, True)], carry=carry)
+        carry = attention_step(query, [far[at], *near], [(by, False), *near_slots], carry=carry)
         carry = attention_step(
             query,
             [far_partner, far_outer[at]],

time: 88.7 us -> 87.9 us (level)
  Pallas kernels: 8.96 us -> 6.88 us
  waiting for transfers between devices: 27.5 us -> 28.7 us
    pallas_call x4 -> x3, Pallas kernels: 5.01 us -> 2.93 us  [attention_step(): pl.pallas_call(functools.partial(attend_body, tuple(slots), bool(text), b...]
    ppermute x2, waiting for transfers between devices: 1.24 us -> 2.48 us  [the longest x1 2.48 us: attention_rows(): lax.ppermute(pair, 'grid', filled(over, devices))]
  transfers between devices with their start and end apart: 23 -> 23, of which waited for: 7 -> 7; matrix products, arithmetic and copies ran while one was open for 2% -> 2% of each run, Pallas kernels for 8% -> 6%
where the time goes in v2:
time: 87.9 us; the launch traced here: 87.6 us
  starting transfers between devices  47.4 us (54%)
  waiting for transfers between devices  28.7 us (33%)
  Pallas kernels  6.88 us (8%)
  local copies, waits for them, and re-layouts  3.59 us (4%)
  between operations  0.96 us (1%)
    ppermute x4, waiting for transfers between devices, send_output_weight(): pieces.append(lax.ppermute(output_weight, ('grid', 'tp'), pairs))  17.5 us
    ppermute x4, starting transfers between devices, send_output_weight(): pieces.append(lax.ppermute(output_weight, ('grid', 'tp'), pairs))  13.4 us
    ppermute x3, starting transfers between devices, local(): lax.ppermute(attention, 'tp', [(at, at ^ by) for at in range(groups)])  6.77 us
    ppermute x3, starting transfers between devices, project(): lax.ppermute(query_weight, 'grid', [(at, (at + 2 * turn) % devices) for a...  6.28 us
    ppermute x3, waiting for transfers between devices, local(): lax.ppermute(attention, 'tp', [(at, at ^ by) for at in range(groups)])  5.51 us
    ppermute x1, starting transfers between devices, attention_rows(): near_outer = lax.ppermute(pair, 'grid', filled(outer, devices))  4.06 us
    ppermute x1, starting transfers between devices, attention_rows(): lax.ppermute(pair, 'grid', filled(over, devices))  3.99 us
    ppermute x1, starting transfers between devices, project(): above = lax.ppermute(pair_weight, 'grid', down)  3.93 us
  transfers between devices with their start and end apart: 23, of which 7 were waited for; matrix products, arithmetic and copies ran while one was open for 2% of the time, Pallas kernels for 6%

profile of v2, /device:TPU:10, one launch (start us, length us, event | category | flops | bytes accessed | tf_op | source)
XLA Modules:
  0.0 87.6 jit_solution(11914946025746816152)
XLA Ops:
  0.0 0.9 %slice.7.refs_0_ = bf16[384,256]{1,0:T(8,128)(2,1)S(1)} slice(bf16[384,384]{1,0:T(8,128)(2,1)} %param.7), slice={[0:384], [128:384]} | slice | bytes 393216 | tf_op jit(solution)/shard_map/slice | solution.py:142
  0.9 2.7 %collective-permute-start.5 = (bf16[384,256]{1,0:T(8,128)(2,1)S(1)}, bf16[384,256]{1,0:T(8,128)(2,1)S(1)}, u32[]{:S(2)}, u32[]{:S(2)}) collective-permute-start(bf16[384,256]{1,0:T(8,128)(2,1)S(1)} %slice.7.refs_0_), channel_id=1, source_target_pairs={{0,16},{4,20},{8,24},{12,28},{16,0},{20,4},{24,8},{28,12},{1,17},{... | collective-permute-start | bytes 589832 | tf_op jit(solution)/shard_map/ppermute | solution.py:143
  3.6 1.9 %collective-permute-start.7 = (bf16[384,256]{1,0:T(8,128)(2,1)S(1)}, bf16[384,256]{1,0:T(8,128)(2,1)S(1)}, u32[]{:S(2)}, u32[]{:S(2)}) collective-permute-start(bf16[384,256]{1,0:T(8,128)(2,1)S(1)} %slice.7.refs_0_), channel_id=1, source_target_pairs={{0,8},{4,12},{8,16},{12,20},{16,24},{20,28},{1,9},{5,13},{9,17},{1... | collective-permute-start | bytes 589832 | tf_op jit(solution)/shard_map/ppermute | solution.py:144
  5.5 3.9 %collective-permute-start.8 = (bf16[384,256]{1,0:T(8,128)(2,1)S(1)}, bf16[384,256]{1,0:T(8,128)(2,1)S(1)}, u32[]{:S(2)}, u32[]{:S(2)}) collective-permute-start(bf16[384,256]{1,0:T(8,128)(2,1)S(1)} %slice.7.refs_0_), channel_id=1, source_target_pairs={{8,0},{12,4},{16,8},{20,12},{24,16},{28,20},{9,1},{13,5},{17,9},{2... | collective-permute-start | bytes 589832 | tf_op jit(solution)/shard_map/ppermute | solution.py:145
  9.5 3.2 %collective-permute-done.5.refs_1_ = bf16[384,256]{1,0:T(8,128)(2,1)S(1)} collective-permute-done((bf16[384,256]{1,0:T(8,128)(2,1)S(1)}, bf16[384,256]{1,0:T(8,128)(2,1)S(1)}, u32[]{:S(2)}, u32[]{:S(2)}) %collective-permute-start.5) | collective-permute-done | bytes 196640 | tf_op jit(solution)/shard_map/ppermute | solution.py:143
  12.6 3.6 %collective-permute-start.6 = (bf16[384,256]{1,0:T(8,128)(2,1)S(1)}, bf16[384,256]{1,0:T(8,128)(2,1)S(1)}, u32[]{:S(2)}, u32[]{:S(2)}) collective-permute-start(bf16[384,256]{1,0:T(8,128)(2,1)S(1)} %collective-permute-done.5.refs_1_), channel_id=1, source_target_pairs={{8,0},{12,4},{16,24},{20,28},{9,1},{13,5},{17,25},{21,29},{10,2},{... | collective-permute-start | bytes 589832 | tf_op jit(solution)/shard_map/ppermute | solution.py:147
  16.3 1.6 %collective-permute-start.18 = (bf16[128,384]{1,0:T(8,128)(2,1)}, bf16[128,384]{1,0:T(8,128)(2,1)S(1)}, u32[]{:S(2)}, u32[]{:S(2)}) collective-permute-start(bf16[128,384]{1,0:T(8,128)(2,1)} %param.11), channel_id=1, source_target_pairs={{0,0},{1,8},{2,16},{3,24},{4,4},{5,12},{6,20},{7,28},{8,1},{9,9},{... | collective-permute-start | bytes 294920 | tf_op jit(solution)/shard_map/ppermute | solution.py:430
  17.8 1.7 %copy-done = bf16[384,3072]{1,0:T(8,128)(2,1)S(1)} copy-done((bf16[384,3072]{1,0:T(8,128)(2,1)S(1)}, bf16[384,3072]{1,0:T(8,128)(2,1)}, u32[]{:S(2)}) %copy-start) | copy-done | bytes 2359320
  21.9 3.3 %collective-permute-start.1 = (bf16[384,128]{1,0:T(8,128)(2,1)S(1)}, bf16[384,128]{1,0:T(8,128)(2,1)S(1)}, u32[]{:S(2)}, u32[]{:S(2)}) collective-permute-start(bf16[384,128]{1,0:T(8,128)(2,1)S(1)} %slice.6.refs_0_), channel_id=1, source_target_pairs={{0,8},{4,12},{8,16},{12,20},{16,24},{20,28},{24,0},{28,4},{1,9},{5... | collective-permute-start | bytes 294920 | tf_op jit(solution)/shard_map/ppermute | solution.py:149
  25.3 1.1 %collective-permute-start.2 = (bf16[384,128]{1,0:T(8,128)(2,1)S(1)}, bf16[384,128]{1,0:T(8,128)(2,1)S(1)}, u32[]{:S(2)}, u32[]{:S(2)}) collective-permute-start(bf16[384,128]{1,0:T(8,128)(2,1)S(1)} %slice.6.refs_0_), channel_id=1, source_target_pairs={{0,16},{4,20},{8,24},{12,28},{16,0},{20,4},{24,8},{28,12},{1,17},{... | collective-permute-start | bytes 294920 | tf_op jit(solution)/shard_map/ppermute | solution.py:149
  26.4 1.9 %collective-permute-start.3 = (bf16[384,128]{1,0:T(8,128)(2,1)S(1)}, bf16[384,128]{1,0:T(8,128)(2,1)S(1)}, u32[]{:S(2)}, u32[]{:S(2)}) collective-permute-start(bf16[384,128]{1,0:T(8,128)(2,1)S(1)} %slice.6.refs_0_), channel_id=1, source_target_pairs={{0,24},{4,28},{8,0},{12,4},{16,8},{20,12},{24,16},{28,20},{1,25},{... | collective-permute-start | bytes 294920 | tf_op jit(solution)/shard_map/ppermute | solution.py:149
  29.0 9.5 %collective-permute-done.19 = bf16[128,384]{1,0:T(8,128)(2,1)S(1)} collective-permute-done((bf16[128,384]{1,0:T(8,128)(2,1)S(1)}, bf16[128,384]{1,0:T(8,128)(2,1)S(1)}, u32[]{:S(2)}, u32[]{:S(2)}) %collective-permute-start.19) | collective-permute-done | bytes 98336 | tf_op jit(solution)/shard_map/ppermute | solution.py:430
  38.5 5.1 %collective-permute-start.20 = (bf16[128,384]{1,0:T(8,128)(2,1)S(1)}, bf16[128,384]{1,0:T(8,128)(2,1)S(1)}, u32[]{:S(2)}, u32[]{:S(2)}) collective-permute-start(bf16[128,384]{1,0:T(8,128)(2,1)S(1)} %copy-done.3), channel_id=1, source_target_pairs={{0,16},{1,24},{2,0},{3,8},{4,20},{5,28},{6,4},{7,12},{8,17},{9,25}... | collective-permute-start | bytes 294920 | tf_op jit(solution)/shard_map/ppermute | solution.py:430
  43.6 4.3 %collective-permute-done.20 = bf16[128,384]{1,0:T(8,128)(2,1)S(1)} collective-permute-done((bf16[128,384]{1,0:T(8,128)(2,1)S(1)}, bf16[128,384]{1,0:T(8,128)(2,1)S(1)}, u32[]{:S(2)}, u32[]{:S(2)}) %collective-permute-start.20) | collective-permute-done | bytes 98336 | tf_op jit(solution)/shard_map/ppermute | solution.py:430
  47.9 6.0 %collective-permute-start.21 = (bf16[128,384]{1,0:T(8,128)(2,1)S(1)}, bf16[128,384]{1,0:T(8,128)(2,1)S(1)}, u32[]{:S(2)}, u32[]{:S(2)}) collective-permute-start(bf16[128,384]{1,0:T(8,128)(2,1)S(1)} %copy-done.3), channel_id=1, source_target_pairs={{0,24},{1,0},{2,8},{3,16},{4,28},{5,4},{6,12},{7,20},{8,25},{9,1},... | collective-permute-start | bytes 294920 | tf_op jit(solution)/shard_map/ppermute | solution.py:430
  55.0 3.8 %collective-permute-done.21 = bf16[128,384]{1,0:T(8,128)(2,1)S(1)} collective-permute-done((bf16[128,384]{1,0:T(8,128)(2,1)S(1)}, bf16[128,384]{1,0:T(8,128)(2,1)S(1)}, u32[]{:S(2)}, u32[]{:S(2)}) %collective-permute-start.21) | collective-permute-done | bytes 98336 | tf_op jit(solution)/shard_map/ppermute | solution.py:430
  59.4 4.1 %collective-permute-start.13 = (bf16[384,256]{1,0:T(8,128)(2,1)S(1)}, bf16[384,256]{1,0:T(8,128)(2,1)S(1)}, u32[]{:S(2)}, u32[]{:S(2)}) collective-permute-start(bf16[384,256]{1,0:T(8,128)(2,1)S(1)} %shard_map.65.refs_1_), channel_id=1, source_target_pairs={{4,8},{8,4},{20,24},{24,20},{0,0},{12,12},{16,16},{28,28},{5,9},{9... | collective-permute-start | bytes 589832 | tf_op jit(solution)/shard_map/ppermute | solution.py:343
  63.5 4.0 %collective-permute-start.12 = (bf16[384,256]{1,0:T(8,128)(2,1)S(1)}, bf16[384,256]{1,0:T(8,128)(2,1)S(1)}, u32[]{:S(2)}, u32[]{:S(2)}) collective-permute-start(bf16[384,256]{1,0:T(8,128)(2,1)S(1)} %shard_map.65.refs_1_), channel_id=1, source_target_pairs={{4,24},{8,20},{20,8},{24,4},{0,0},{12,12},{16,16},{28,28},{5,25},{... | collective-permute-start | bytes 589832 | tf_op jit(solution)/shard_map/ppermute | solution.py:344
  68.4 1.1 %attention_step.3 = (f32[384,128]{1,0:T(8,128)S(1)}, f32[384,128]{1,0:T(8,128)S(1)}, f32[384,128]{1,0:T(8,128)S(1)}) custom-call(bf16[384,128]{1,0:T(8,128)(2,1)S(1)} %shard_map.64.refs_0_, bf16[384,256]{1,0:T(8,128)(2,1)S(1)} %shard_map.65.refs_1_, bf16[384,256]{1,0:T(8,128)(2,1)S(1)} %collective-permute-done.14.refs_2_, s32[1]{0:T(128)S(6)} %copy.10.refs_3_, ...), custom_call_target="tpu_custom_call" | custom-call | flops 150994944 | bytes 393216 | tf_op jit(solution)/shard_map/attention_step/pallas_call | solution.py:305
  70.4 2.5 %collective-permute-done.12.refs_2_ = bf16[384,256]{1,0:T(8,128)(2,1)S(1)} collective-permute-done((bf16[384,256]{1,0:T(8,128)(2,1)S(1)}, bf16[384,256]{1,0:T(8,128)(2,1)S(1)}, u32[]{:S(2)}, u32[]{:S(2)}) %collective-permute-start.12) | collective-permute-done | bytes 196640 | tf_op jit(solution)/shard_map/ppermute | solution.py:344
  73.9 6.7 %collective-permute-start.16 = (bf16[384,128]{1,0:T(8,128)(2,1)S(1)}, bf16[384,128]{1,0:T(8,128)(2,1)S(1)}, u32[]{:S(2)}, u32[]{:S(2)}) collective-permute-start(bf16[384,128]{1,0:T(8,128)(2,1)S(1)} %attention_step.5.refs_0_), channel_id=1, source_target_pairs={{0,2},{1,3},{2,0},{3,1},{4,6},{5,7},{6,4},{7,5},{8,10},{9,11},{10,... | collective-permute-start | bytes 294920 | tf_op jit(solution)/shard_map/ppermute | solution.py:448
  80.6 2.6 %collective-permute-done.16.refs_2_ = bf16[384,128]{1,0:T(8,128)(2,1)S(1)} collective-permute-done((bf16[384,128]{1,0:T(8,128)(2,1)S(1)}, bf16[384,128]{1,0:T(8,128)(2,1)S(1)}, u32[]{:S(2)}, u32[]{:S(2)}) %collective-permute-start.16) | collective-permute-done | bytes 98336 | tf_op jit(solution)/shard_map/ppermute | solution.py:448
  83.2 2.9 %collective-permute-done.17.refs_3_ = bf16[384,128]{1,0:T(8,128)(2,1)S(1)} collective-permute-done((bf16[384,128]{1,0:T(8,128)(2,1)S(1)}, bf16[384,128]{1,0:T(8,128)(2,1)S(1)}, u32[]{:S(2)}, u32[]{:S(2)}) %collective-permute-start.17) | collective-permute-done | bytes 98336 | tf_op jit(solution)/shard_map/ppermute | solution.py:448
  86.1 1.5 %output_product.1 = bf16[384,768]{1,0:T(8,128)(2,1)} custom-call(bf16[384,128]{1,0:T(8,128)(2,1)S(1)} %attention_step.5.refs_0_, bf16[384,128]{1,0:T(8,128)(2,1)S(1)} %collective-permute-done.15.refs_1_, bf16[384,128]{1,0:T(8,128)(2,1)S(1)} %collective-permute-done.16.refs_2_, bf16[384,128]{1,0:T(8,128)(2,1)S(1)} %collective-permute-done.17.refs_3_, ...), custom_call_target="tpu_custom_call" | custom-call | flops 301989888 | bytes 1376256 | tf_op jit(solution)/shard_map/output_product/pallas_call | solution.py:395
  (46 shorter events, 7.0 us)
Async XLA Ops:
  0.0 17.8 %collective-permute-start = (bf16[384,3072]{1,0:T(8,128)(2,1)}, bf16[384,3072]{1,0:T(8,128)(2,1)S(1)}, u32[]{:S(2)}, u32[]{:S(2)}) collective-permute-start(bf16[384,3072]{1,0:T(8,128)(2,1)} %latents_ref.7), channel_id=1, source_target_pairs={{0,4},{4,0},{8,12},{12,8},{16,20},{20,16},{24,28},{28,24},{1,5},{5... | collective-permute-start | bytes 7077896 | tf_op jit(solution)/shard_map/ppermute | solution.py:146
  0.9 11.7 %collective-permute-start.5 = (bf16[384,256]{1,0:T(8,128)(2,1)S(1)}, bf16[384,256]{1,0:T(8,128)(2,1)S(1)}, u32[]{:S(2)}, u32[]{:S(2)}) collective-permute-start(bf16[384,256]{1,0:T(8,128)(2,1)S(1)} %slice.7.refs_0_), channel_id=1, source_target_pairs={{0,16},{4,20},{8,24},{12,28},{16,0},{20,4},{24,8},{28,12},{1,17},{... | collective-permute-start | bytes 589832 | tf_op jit(solution)/shard_map/ppermute | solution.py:143
  3.6 16.5 %collective-permute-start.7 = (bf16[384,256]{1,0:T(8,128)(2,1)S(1)}, bf16[384,256]{1,0:T(8,128)(2,1)S(1)}, u32[]{:S(2)}, u32[]{:S(2)}) collective-permute-start(bf16[384,256]{1,0:T(8,128)(2,1)S(1)} %slice.7.refs_0_), channel_id=1, source_target_pairs={{0,8},{4,12},{8,16},{12,20},{16,24},{20,28},{1,9},{5,13},{9,17},{1... | collective-permute-start | bytes 589832 | tf_op jit(solution)/shard_map/ppermute | solution.py:144
  5.5 14.6 %collective-permute-start.8 = (bf16[384,256]{1,0:T(8,128)(2,1)S(1)}, bf16[384,256]{1,0:T(8,128)(2,1)S(1)}, u32[]{:S(2)}, u32[]{:S(2)}) collective-permute-start(bf16[384,256]{1,0:T(8,128)(2,1)S(1)} %slice.7.refs_0_), channel_id=1, source_target_pairs={{8,0},{12,4},{16,8},{20,12},{24,16},{28,20},{9,1},{13,5},{17,9},{2... | collective-permute-start | bytes 589832 | tf_op jit(solution)/shard_map/ppermute | solution.py:145
  12.6 8.3 %collective-permute-start.6 = (bf16[384,256]{1,0:T(8,128)(2,1)S(1)}, bf16[384,256]{1,0:T(8,128)(2,1)S(1)}, u32[]{:S(2)}, u32[]{:S(2)}) collective-permute-start(bf16[384,256]{1,0:T(8,128)(2,1)S(1)} %collective-permute-done.5.refs_1_), channel_id=1, source_target_pairs={{8,0},{12,4},{16,24},{20,28},{9,1},{13,5},{17,25},{21,29},{10,2},{... | collective-permute-start | bytes 589832 | tf_op jit(solution)/shard_map/ppermute | solution.py:147
  16.3 12.0 %collective-permute-start.18 = (bf16[128,384]{1,0:T(8,128)(2,1)}, bf16[128,384]{1,0:T(8,128)(2,1)S(1)}, u32[]{:S(2)}, u32[]{:S(2)}) collective-permute-start(bf16[128,384]{1,0:T(8,128)(2,1)} %param.11), channel_id=1, source_target_pairs={{0,0},{1,8},{2,16},{3,24},{4,4},{5,12},{6,20},{7,28},{8,1},{9,9},{... | collective-permute-start | bytes 294920 | tf_op jit(solution)/shard_map/ppermute | solution.py:430
  21.0 33.8 %collective-permute-start.9 = (f32[384,256]{1,0:T(8,128)S(1)}, f32[384,256]{1,0:T(8,128)S(1)}, u32[]{:S(2)}, u32[]{:S(2)}) collective-permute-start(f32[384,256]{1,0:T(8,128)S(1)} %get-tuple-element.26), channel_id=1, source_target_pairs={{0,4},{4,0},{8,12},{12,8},{16,20},{20,16},{24,28},{28,24},{1,5},{5... | collective-permute-start | bytes 1179656 | tf_op jit(solution)/shard_map/ppermute | solution.py:176
  21.9 31.9 %collective-permute-start.1 = (bf16[384,128]{1,0:T(8,128)(2,1)S(1)}, bf16[384,128]{1,0:T(8,128)(2,1)S(1)}, u32[]{:S(2)}, u32[]{:S(2)}) collective-permute-start(bf16[384,128]{1,0:T(8,128)(2,1)S(1)} %slice.6.refs_0_), channel_id=1, source_target_pairs={{0,8},{4,12},{8,16},{12,20},{16,24},{20,28},{24,0},{28,4},{1,9},{5... | collective-permute-start | bytes 294920 | tf_op jit(solution)/shard_map/ppermute | solution.py:149
  25.3 28.6 %collective-permute-start.2 = (bf16[384,128]{1,0:T(8,128)(2,1)S(1)}, bf16[384,128]{1,0:T(8,128)(2,1)S(1)}, u32[]{:S(2)}, u32[]{:S(2)}) collective-permute-start(bf16[384,128]{1,0:T(8,128)(2,1)S(1)} %slice.6.refs_0_), channel_id=1, source_target_pairs={{0,16},{4,20},{8,24},{12,28},{16,0},{20,4},{24,8},{28,12},{1,17},{... | collective-permute-start | bytes 294920 | tf_op jit(solution)/shard_map/ppermute | solution.py:149
  26.4 27.5 %collective-permute-start.3 = (bf16[384,128]{1,0:T(8,128)(2,1)S(1)}, bf16[384,128]{1,0:T(8,128)(2,1)S(1)}, u32[]{:S(2)}, u32[]{:S(2)}) collective-permute-start(bf16[384,128]{1,0:T(8,128)(2,1)S(1)} %slice.6.refs_0_), channel_id=1, source_target_pairs={{0,24},{4,28},{8,0},{12,4},{16,8},{20,12},{24,16},{28,20},{1,25},{... | collective-permute-start | bytes 294920 | tf_op jit(solution)/shard_map/ppermute | solution.py:149
  28.2 10.3 %collective-permute-start.19 = (bf16[128,384]{1,0:T(8,128)(2,1)S(1)}, bf16[128,384]{1,0:T(8,128)(2,1)S(1)}, u32[]{:S(2)}, u32[]{:S(2)}) collective-permute-start(bf16[128,384]{1,0:T(8,128)(2,1)S(1)} %copy-done.3), channel_id=1, source_target_pairs={{0,8},{1,16},{2,24},{3,0},{4,12},{5,20},{6,28},{7,4},{8,9},{9,17},... | collective-permute-start | bytes 294920 | tf_op jit(solution)/shard_map/ppermute | solution.py:430
  38.5 9.3 %collective-permute-start.20 = (bf16[128,384]{1,0:T(8,128)(2,1)S(1)}, bf16[128,384]{1,0:T(8,128)(2,1)S(1)}, u32[]{:S(2)}, u32[]{:S(2)}) collective-permute-start(bf16[128,384]{1,0:T(8,128)(2,1)S(1)} %copy-done.3), channel_id=1, source_target_pairs={{0,16},{1,24},{2,0},{3,8},{4,20},{5,28},{6,4},{7,12},{8,17},{9,25}... | collective-permute-start | bytes 294920 | tf_op jit(solution)/shard_map/ppermute | solution.py:430
  47.9 10.9 %collective-permute-start.21 = (bf16[128,384]{1,0:T(8,128)(2,1)S(1)}, bf16[128,384]{1,0:T(8,128)(2,1)S(1)}, u32[]{:S(2)}, u32[]{:S(2)}) collective-permute-start(bf16[128,384]{1,0:T(8,128)(2,1)S(1)} %copy-done.3), channel_id=1, source_target_pairs={{0,24},{1,0},{2,8},{3,16},{4,28},{5,4},{6,12},{7,20},{8,25},{9,1},... | collective-permute-start | bytes 294920 | tf_op jit(solution)/shard_map/ppermute | solution.py:430
  53.9 14.5 %copy-start.1 = (bf16[256,256]{1,0:T(8,128)(2,1)S(1)}, bf16[256,256]{1,0:T(8,128)(2,1)}, u32[]{:S(2)}) copy-start(bf16[256,256]{1,0:T(8,128)(2,1)} %refs_4_.1) | copy-start | bytes 393220
  54.7 8.8 %collective-permute-start.4 = (f32[384,128]{1,0:T(8,128)S(1)}, f32[384,128]{1,0:T(8,128)S(1)}, u32[]{:S(2)}, u32[]{:S(2)}) collective-permute-start(f32[384,128]{1,0:T(8,128)S(1)} %get-tuple-element.20), channel_id=1, source_target_pairs={{0,4},{4,0},{8,12},{12,8},{16,20},{20,16},{24,28},{28,24},{1,5},{5... | collective-permute-start | bytes 589832 | tf_op jit(solution)/shard_map/ppermute | solution.py:187
  55.0 12.5 %collective-permute-start.10 = (bf16[384,256]{1,0:T(8,128)(2,1)S(1)}, bf16[384,256]{1,0:T(8,128)(2,1)S(1)}, u32[]{:S(2)}, u32[]{:S(2)}) collective-permute-start(bf16[384,256]{1,0:T(8,128)(2,1)S(1)} %shard_map.65.refs_1_), channel_id=1, source_target_pairs={{0,16},{4,20},{8,24},{12,28},{16,0},{20,4},{24,8},{28,12},{1,17},{... | collective-permute-start | bytes 589832 | tf_op jit(solution)/shard_map/ppermute | solution.py:341
  58.8 21.8 %collective-permute-start.22 = (bf16[512,384]{1,0:T(8,128)(2,1)S(1)}, bf16[512,384]{1,0:T(8,128)(2,1)S(1)}, u32[]{:S(2)}, u32[]{:S(2)}) collective-permute-start(bf16[512,384]{1,0:T(8,128)(2,1)S(1)} %constant_dynamic-update-slice_fusion.refs_4_), channel_id=1, source_target_pairs={{0,4},{4,0},{8,12},{12,8},{16,20},{20,16},{24,28},{28,24},{1,5},{5... | collective-permute-start | bytes 1179656 | tf_op jit(solution)/shard_map/ppermute | solution.py:446
  58.9 9.5 %collective-permute-start.14 = (bf16[384,256]{1,0:T(8,128)(2,1)S(1)}, bf16[384,256]{1,0:T(8,128)(2,1)S(1)}, u32[]{:S(2)}, u32[]{:S(2)}) collective-permute-start(bf16[384,256]{1,0:T(8,128)(2,1)S(1)} %shard_map.65.refs_1_), channel_id=1, source_target_pairs={{0,4},{4,0},{8,12},{12,8},{16,20},{20,16},{24,28},{28,24},{1,5},{5... | collective-permute-start | bytes 589832 | tf_op jit(solution)/shard_map/ppermute | solution.py:342
  59.4 10.1 %collective-permute-start.13 = (bf16[384,256]{1,0:T(8,128)(2,1)S(1)}, bf16[384,256]{1,0:T(8,128)(2,1)S(1)}, u32[]{:S(2)}, u32[]{:S(2)}) collective-permute-start(bf16[384,256]{1,0:T(8,128)(2,1)S(1)} %shard_map.65.refs_1_), channel_id=1, source_target_pairs={{4,8},{8,4},{20,24},{24,20},{0,0},{12,12},{16,16},{28,28},{5,9},{9... | collective-permute-start | bytes 589832 | tf_op jit(solution)/shard_map/ppermute | solution.py:343
  63.5 9.4 %collective-permute-start.12 = (bf16[384,256]{1,0:T(8,128)(2,1)S(1)}, bf16[384,256]{1,0:T(8,128)(2,1)S(1)}, u32[]{:S(2)}, u32[]{:S(2)}) collective-permute-start(bf16[384,256]{1,0:T(8,128)(2,1)S(1)} %shard_map.65.refs_1_), channel_id=1, source_target_pairs={{4,24},{8,20},{20,8},{24,4},{0,0},{12,12},{16,16},{28,28},{5,25},{... | collective-permute-start | bytes 589832 | tf_op jit(solution)/shard_map/ppermute | solution.py:344
  67.5 5.4 %collective-permute-start.11 = (bf16[384,256]{1,0:T(8,128)(2,1)S(1)}, bf16[384,256]{1,0:T(8,128)(2,1)S(1)}, u32[]{:S(2)}, u32[]{:S(2)}) collective-permute-start(bf16[384,256]{1,0:T(8,128)(2,1)S(1)} %collective-permute-done.10.refs_1_), channel_id=1, source_target_pairs={{0,4},{4,0},{8,12},{12,8},{16,20},{20,16},{24,28},{28,24},{1,5},{5... | collective-permute-start | bytes 589832 | tf_op jit(solution)/shard_map/ppermute | solution.py:350
  73.8 6.8 %collective-permute-start.15 = (bf16[384,128]{1,0:T(8,128)(2,1)S(1)}, bf16[384,128]{1,0:T(8,128)(2,1)S(1)}, u32[]{:S(2)}, u32[]{:S(2)}) collective-permute-start(bf16[384,128]{1,0:T(8,128)(2,1)S(1)} %attention_step.5.refs_0_), channel_id=1, source_target_pairs={{0,1},{1,0},{2,3},{3,2},{4,5},{5,4},{6,7},{7,6},{8,9},{9,8},{10,11... | collective-permute-start | bytes 294920 | tf_op jit(solution)/shard_map/ppermute | solution.py:448
  73.9 9.3 %collective-permute-start.16 = (bf16[384,128]{1,0:T(8,128)(2,1)S(1)}, bf16[384,128]{1,0:T(8,128)(2,1)S(1)}, u32[]{:S(2)}, u32[]{:S(2)}) collective-permute-start(bf16[384,128]{1,0:T(8,128)(2,1)S(1)} %attention_step.5.refs_0_), channel_id=1, source_target_pairs={{0,2},{1,3},{2,0},{3,1},{4,6},{5,7},{6,4},{7,5},{8,10},{9,11},{10,... | collective-permute-start | bytes 294920 | tf_op jit(solution)/shard_map/ppermute | solution.py:448
  80.6 5.5 %collective-permute-start.17 = (bf16[384,128]{1,0:T(8,128)(2,1)S(1)}, bf16[384,128]{1,0:T(8,128)(2,1)S(1)}, u32[]{:S(2)}, u32[]{:S(2)}) collective-permute-start(bf16[384,128]{1,0:T(8,128)(2,1)S(1)} %attention_step.5.refs_0_), channel_id=1, source_target_pairs={{0,3},{1,2},{2,1},{3,0},{4,7},{5,6},{6,5},{7,4},{8,11},{9,10},{10,... | collective-permute-start | bytes 294920 | tf_op jit(solution)/shard_map/ppermute | solution.py:448
  (3 other events, 10.0 us)

commit v3 on v2

--- a/solution.py
+++ b/solution.py
@@ -133,18 +133,13 @@
     every = range(devices)
     swap = [(at, at ^ 1) for at in every]
     across = [(at, at ^ chips) for at in every]
-    up = [(at, at + 2) for at in every if at + 2 < devices]
-    down = [(at, at - 2) for at in every if at >= 2]
-    outward = [(at, at - 2) for at in (2, 3)] + [
-        (at, at + 2) for at in (devices - 4, devices - 3)
-    ]
+    beside = [(at, at ^ 2) for at in every]
     half = chips // 2
     pair_weight, query_weight = input_weight[:, head_size:], input_weight[:, :head_size]
     far = lax.ppermute(pair_weight, "grid", across)
-    below = lax.ppermute(pair_weight, "grid", up)
-    above = lax.ppermute(pair_weight, "grid", down)
+    near = lax.ppermute(pair_weight, "grid", beside)
     partner_latents = lax.ppermute(latents, "grid", swap)
-    relayed = lax.ppermute(far, "grid", outward)
+    relayed = lax.ppermute(far, "grid", beside)
     query_shards = [query_weight] + [
         lax.ppermute(query_weight, "grid", [(at, (at + 2 * turn) % devices) for at in every])
         for turn in range(1, chips)
@@ -152,26 +147,12 @@
     carry = partial_product(
         latents,
         partner_latents,
-        [pair_weight, far],
-        [(lambda chip: chip, None), (lambda chip: lax.rem(chip + half, chips), None)],
+        [pair_weight, far, near],
+        [(lambda chip: chip, None), (lambda chip: chip ^ half, None), (lambda chip: chip ^ 1, None)],
         (),
     )
-    carry = partial_product(
-        latents,
-        partner_latents,
-        [below, above],
-        [
-            (lambda chip: chip - 1, lambda chip, chips: chip > 0),
-            (lambda chip: chip + 1, lambda chip, chips: chip < chips - 1),
-        ],
-        carry,
-    )
     mine, other = partial_product(
-        latents,
-        partner_latents,
-        [relayed],
-        [(lambda chip: chips - 1 - chip, lambda chip, chips: (chip == 0) | (chip == chips - 1))],
-        carry,
+        latents, partner_latents, [relayed], [(lambda chip: chip ^ half ^ 1, None)], carry
     )
     pair = finish(finish_keys, mine, lax.ppermute(other, "grid", swap), norm_gains)
     mine, other = partial_product(
@@ -316,6 +297,84 @@
     )(query, *pairs, *text, *carry)
 
 
+def reply_body(query_ref, own_ref, partner_ref, outer_ref, out_ref, *, factor):
+    rows, head_size = query_ref.shape
+    beyond = outer_height(lax.rem(lax.axis_index("grid"), GRID_H))
+    outer_ok = (beyond >= 0) & (beyond < GRID_H)
+
+    def tiles(refs):
+        return [(ref[:, :head_size], ref[:, head_size:], None) for ref in refs]
+
+    def finish(refs):
+        top, total, mixed = attend(None, query_ref[...], tiles(refs), factor)
+        out_ref[:rows] = (mixed / total).astype(BF16)
+        level = top + jnp.log(total) * LOG2E
+        square = (head_size, head_size)
+        diagonal = lax.broadcasted_iota(jnp.int32, square, 0) == lax.broadcasted_iota(
+            jnp.int32, square, 1
+        )
+        tail = (out_ref.shape[0] - rows, head_size)
+        line = lax.broadcasted_iota(jnp.int32, tail, 0)
+        terms = jnp.zeros(tail, F32)
+        for at in range(rows // head_size):
+            block = level[at * head_size : (at + 1) * head_size]
+            rest = jnp.where(diagonal, block, 0.0).sum(0, keepdims=True)
+            for part in range(3):
+                term = rest.astype(BF16).astype(F32)
+                terms = jnp.where(line == 3 * at + part, term, terms)
+                rest = rest - term
+        out_ref[rows:] = terms.astype(BF16)
+
+    @pl.when(outer_ok)
+    def _():
+        finish([own_ref, partner_ref, outer_ref])
+
+    @pl.when(jnp.logical_not(outer_ok))
+    def _():
+        finish([own_ref, partner_ref])
+
+
+def reply(query, tiles):
+    rows, head_size = query.shape
+    tail = -(-3 * (rows // head_size) // 16) * 16
+    return pl.pallas_call(
+        functools.partial(reply_body, factor=head_size ** (-0.5) * LOG2E),
+        out_shape=shape_of((rows + tail, head_size), BF16),
+        in_specs=[VMEM] * (1 + len(tiles)),
+        out_specs=VMEM,
+        cost_estimate=cost(12 * rows * rows * head_size, 8 * rows * head_size, 3 * rows * rows),
+        compiler_params=GRANT,
+        name="reply",
+    )(query, *tiles)
+
+
+def merge_body(top_ref, total_ref, mixed_ref, reply_ref, out_ref):
+    rows, head_size = out_ref.shape
+    terms = reply_ref[rows:].astype(F32)
+    for at in range(rows // head_size):
+        here = slice(at * head_size, (at + 1) * head_size)
+        line = terms[3 * at : 3 * at + 1] + terms[3 * at + 1 : 3 * at + 2]
+        line = line + terms[3 * at + 2 : 3 * at + 3]
+        level = jnp.transpose(jnp.broadcast_to(line, (head_size, head_size)))
+        top = jnp.maximum(top_ref[here], level)
+        mine, theirs = jnp.exp2(top_ref[here] - top), jnp.exp2(level - top)
+        mixed = mixed_ref[here] * mine + reply_ref[here].astype(F32) * theirs
+        out_ref[here] = (mixed / (total_ref[here] * mine + theirs)).astype(BF16)
+
+
+def merge(state, replied):
+    rows, head_size = state[2].shape
+    return pl.pallas_call(
+        merge_body,
+        out_shape=shape_of((rows, head_size), BF16),
+        in_specs=[VMEM] * 4,
+        out_specs=VMEM,
+        cost_estimate=cost(8 * rows * head_size, 16 * rows * head_size, 2 * rows),
+        compiler_params=GRANT,
+        name="merge",
+    )(*state, replied)
+
+
 def attention_rows(query, pair, text_pairs, norm_gains, text_count):
     devices = lax.axis_size("grid")
     times = devices // GRID_H
@@ -338,6 +397,20 @@
         plans = [(by, later(same, by), later(outer, by)) for by in (1, -1)]
     else:
         plans = []
+    if times == 2:
+        across = plans[0][1]
+        asked = lax.ppermute(query, "grid", across)
+        partner = lax.ppermute(pair, "grid", swap)
+        near_outer = lax.ppermute(pair, "grid", filled(outer, devices))
+        tiles = [pair, partner, near_outer]
+        replied = lax.ppermute(reply(asked, tiles), "grid", across)
+        state = attention_step(
+            query,
+            tiles,
+            [(None, False), (None, False), (None, True)],
+            text=(text_count, text_pairs, norm_gains),
+        )
+        return merge(state, replied)
     far = [lax.ppermute(pair, "grid", along) for _, along, _ in plans]
     partner = lax.ppermute(pair, "grid", swap)
     near_outer = lax.ppermute(pair, "grid", filled(outer, devices))

time: 87.9 us -> 80.2 us (0.912)
  the two profiles are of different devices: /device:TPU:10 before, /device:TPU:0 now
where the time goes in v3:
time: 80.2 us; the launch traced here: 80 us
  waiting for transfers between devices  39 us (49%)
  starting transfers between devices  30.6 us (38%)
  Pallas kernels  5.93 us (7%)
  local copies, waits for them, and re-layouts  3.59 us (4%)
  between operations  0.85 us (1%)
    ppermute x4, starting transfers between devices, send_output_weight(): pieces.append(lax.ppermute(output_weight, ('grid', 'tp'), pairs))  13.1 us
    ppermute x1, waiting for transfers between devices, project(): far = lax.ppermute(pair_weight, 'grid', across)  8.31 us
    ppermute x4, waiting for transfers between devices, send_output_weight(): pieces.append(lax.ppermute(output_weight, ('grid', 'tp'), pairs))  7.68 us
    ppermute x1, waiting for transfers between devices, project(): relayed = lax.ppermute(far, 'grid', beside)  6.9 us
    ppermute x1, waiting for transfers between devices, attention_rows(): asked = lax.ppermute(query, 'grid', across)  6.19 us
    ppermute x1, waiting for transfers between devices, attention_rows(): replied = lax.ppermute(reply(asked, tiles), 'grid', across)  5.38 us
    ppermute x3, waiting for transfers between devices, local(): lax.ppermute(attention, 'tp', [(at, at ^ by) for at in range(groups)])  4.51 us
    ppermute x3, starting transfers between devices, local(): lax.ppermute(attention, 'tp', [(at, at ^ by) for at in range(groups)])  4.21 us
  transfers between devices with their start and end apart: 21, of which 9 were waited for; matrix products, arithmetic and copies ran while one was open for 2% of the time, Pallas kernels for 6%

profile of v3, /device:TPU:0, one launch (start us, length us, event | category | flops | bytes accessed | tf_op | source)
XLA Modules:
  0.0 80.0 jit_solution(17705758689016331931)
XLA Ops:
  0.5 0.9 %slice.7.refs_0_ = bf16[384,256]{1,0:T(8,128)(2,1)S(1)} slice(bf16[384,384]{1,0:T(8,128)(2,1)} %param.7), slice={[0:384], [128:384]} | slice | bytes 393216 | tf_op jit(solution)/shard_map/slice | solution.py:138
  1.4 3.6 %collective-permute-start.5 = (bf16[384,256]{1,0:T(8,128)(2,1)S(1)}, bf16[384,256]{1,0:T(8,128)(2,1)S(1)}, u32[]{:S(2)}, u32[]{:S(2)}) collective-permute-start(bf16[384,256]{1,0:T(8,128)(2,1)S(1)} %slice.7.refs_0_), channel_id=1, source_target_pairs={{0,16},{4,20},{8,24},{12,28},{16,0},{20,4},{24,8},{28,12},{1,17},{... | collective-permute-start | bytes 589832 | tf_op jit(solution)/shard_map/ppermute | solution.py:139
  5.1 1.6 %collective-permute-start.7 = (bf16[384,256]{1,0:T(8,128)(2,1)S(1)}, bf16[384,256]{1,0:T(8,128)(2,1)S(1)}, u32[]{:S(2)}, u32[]{:S(2)}) collective-permute-start(bf16[384,256]{1,0:T(8,128)(2,1)S(1)} %slice.7.refs_0_), channel_id=1, source_target_pairs={{0,8},{4,12},{8,0},{12,4},{16,24},{20,28},{24,16},{28,20},{1,9},{5... | collective-permute-start | bytes 589832 | tf_op jit(solution)/shard_map/ppermute | solution.py:140
  6.7 8.3 %collective-permute-done.5.refs_1_ = bf16[384,256]{1,0:T(8,128)(2,1)S(1)} collective-permute-done((bf16[384,256]{1,0:T(8,128)(2,1)S(1)}, bf16[384,256]{1,0:T(8,128)(2,1)S(1)}, u32[]{:S(2)}, u32[]{:S(2)}) %collective-permute-start.5) | collective-permute-done | bytes 196640 | tf_op jit(solution)/shard_map/ppermute | solution.py:139
  15.6 1.5 %collective-permute-start.16 = (bf16[128,384]{1,0:T(8,128)(2,1)}, bf16[128,384]{1,0:T(8,128)(2,1)S(1)}, u32[]{:S(2)}, u32[]{:S(2)}) collective-permute-start(bf16[128,384]{1,0:T(8,128)(2,1)} %param.11), channel_id=1, source_target_pairs={{0,0},{1,8},{2,16},{3,24},{4,4},{5,12},{6,20},{7,28},{8,1},{9,9},{... | collective-permute-start | bytes 294920 | tf_op jit(solution)/shard_map/ppermute | solution.py:503
  17.2 1.7 %copy-done = bf16[384,3072]{1,0:T(8,128)(2,1)S(1)} copy-done((bf16[384,3072]{1,0:T(8,128)(2,1)S(1)}, bf16[384,3072]{1,0:T(8,128)(2,1)}, u32[]{:S(2)}) %copy-start) | copy-done | bytes 2359320
  19.6 6.9 %collective-permute-done.6.refs_0_ = bf16[384,256]{1,0:T(8,128)(2,1)S(1)} collective-permute-done((bf16[384,256]{1,0:T(8,128)(2,1)S(1)}, bf16[384,256]{1,0:T(8,128)(2,1)S(1)}, u32[]{:S(2)}, u32[]{:S(2)}) %collective-permute-start.6) | collective-permute-done | bytes 196640 | tf_op jit(solution)/shard_map/ppermute | solution.py:142
  27.0 0.9 %slice.6.refs_0_ = bf16[384,128]{1,0:T(8,128)(2,1)S(1)} slice(bf16[384,384]{1,0:T(8,128)(2,1)} %param.7), slice={[0:384], [0:128]} | slice | bytes 196608 | tf_op jit(solution)/shard_map/slice | solution.py:138
  28.0 3.7 %collective-permute-start.3 = (bf16[384,128]{1,0:T(8,128)(2,1)S(1)}, bf16[384,128]{1,0:T(8,128)(2,1)S(1)}, u32[]{:S(2)}, u32[]{:S(2)}) collective-permute-start(bf16[384,128]{1,0:T(8,128)(2,1)S(1)} %slice.6.refs_0_), channel_id=1, source_target_pairs={{0,24},{4,28},{8,0},{12,4},{16,8},{20,12},{24,16},{28,20},{1,25},{... | collective-permute-start | bytes 294920 | tf_op jit(solution)/shard_map/ppermute | solution.py:144
  32.3 5.5 %collective-permute-done.17 = bf16[128,384]{1,0:T(8,128)(2,1)S(1)} collective-permute-done((bf16[128,384]{1,0:T(8,128)(2,1)S(1)}, bf16[128,384]{1,0:T(8,128)(2,1)S(1)}, u32[]{:S(2)}, u32[]{:S(2)}) %collective-permute-start.17) | collective-permute-done | bytes 98336 | tf_op jit(solution)/shard_map/ppermute | solution.py:503
  37.8 6.3 %collective-permute-start.18 = (bf16[128,384]{1,0:T(8,128)(2,1)S(1)}, bf16[128,384]{1,0:T(8,128)(2,1)S(1)}, u32[]{:S(2)}, u32[]{:S(2)}) collective-permute-start(bf16[128,384]{1,0:T(8,128)(2,1)S(1)} %copy-done.3), channel_id=1, source_target_pairs={{0,16},{1,24},{2,0},{3,8},{4,20},{5,28},{6,4},{7,12},{8,17},{9,25}... | collective-permute-start | bytes 294920 | tf_op jit(solution)/shard_map/ppermute | solution.py:503
  44.2 4.7 %collective-permute-start.19 = (bf16[128,384]{1,0:T(8,128)(2,1)S(1)}, bf16[128,384]{1,0:T(8,128)(2,1)S(1)}, u32[]{:S(2)}, u32[]{:S(2)}) collective-permute-start(bf16[128,384]{1,0:T(8,128)(2,1)S(1)} %copy-done.3), channel_id=1, source_target_pairs={{0,24},{1,0},{2,8},{3,16},{4,28},{5,4},{6,12},{7,20},{8,25},{9,1},... | collective-permute-start | bytes 294920 | tf_op jit(solution)/shard_map/ppermute | solution.py:503
  49.7 2.2 %collective-permute-done.18 = bf16[128,384]{1,0:T(8,128)(2,1)S(1)} collective-permute-done((bf16[128,384]{1,0:T(8,128)(2,1)S(1)}, bf16[128,384]{1,0:T(8,128)(2,1)S(1)}, u32[]{:S(2)}, u32[]{:S(2)}) %collective-permute-start.18) | collective-permute-done | bytes 98336 | tf_op jit(solution)/shard_map/ppermute | solution.py:503
  53.6 1.6 %collective-permute-start.11 = (bf16[384,128]{1,0:T(8,128)(2,1)S(1)}, bf16[384,128]{1,0:T(8,128)(2,1)S(1)}, u32[]{:S(2)}, u32[]{:S(2)}) collective-permute-start(bf16[384,128]{1,0:T(8,128)(2,1)S(1)} %shard_map.64.refs_0_), channel_id=1, source_target_pairs={{0,16},{4,20},{8,24},{12,28},{16,0},{20,4},{24,8},{28,12},{1,17},{... | collective-permute-start | bytes 294920 | tf_op jit(solution)/shard_map/ppermute | solution.py:402
  55.2 6.2 %collective-permute-done.11.query_ref = bf16[384,128]{1,0:T(8,128)(2,1)S(1)} collective-permute-done((bf16[384,128]{1,0:T(8,128)(2,1)S(1)}, bf16[384,128]{1,0:T(8,128)(2,1)S(1)}, u32[]{:S(2)}, u32[]{:S(2)}) %collective-permute-start.11) | collective-permute-done | bytes 98336 | tf_op jit(solution)/shard_map/ppermute | solution.py:402
  61.4 0.9 %reply.1 = bf16[400,128]{1,0:T(8,128)(2,1)S(1)} custom-call(bf16[384,128]{1,0:T(8,128)(2,1)S(1)} %collective-permute-done.11.query_ref, bf16[384,256]{1,0:T(8,128)(2,1)S(1)} %shard_map.65.refs_1_.own_ref, bf16[384,256]{1,0:T(8,128)(2,1)S(1)} %collective-permute-done.9.refs_2_.partner_ref, bf16[384,256]{1,0:T(8,128)(2,1)S(1)} %collective-permute-done.10.refs_3_.outer_ref), custom_call_target="tpu_custom_call" | custom-call | flops 226492416 | bytes 393216 | tf_op jit(solution)/shard_map/reply/pallas_call | solution.py:340
  63.0 1.2 %attention_step.1 = (f32[384,128]{1,0:T(8,128)S(1)}, f32[384,128]{1,0:T(8,128)S(1)}, f32[384,128]{1,0:T(8,128)S(1)}) custom-call(bf16[384,128]{1,0:T(8,128)(2,1)S(1)} %shard_map.64.refs_0_, bf16[384,256]{1,0:T(8,128)(2,1)S(1)} %shard_map.65.refs_1_.own_ref, bf16[384,256]{1,0:T(8,128)(2,1)S(1)} %collective-permute-done.9.refs_2_.partner_ref, ...), custom_call_target="tpu_custom_call" | custom-call | flops 226492416 | bytes 589824 | tf_op jit(solution)/shard_map/attention_step/pallas_call | solution.py:286
  64.2 5.4 %collective-permute-done.12.reply_ref = bf16[400,128]{1,0:T(8,128)(2,1)S(1)} collective-permute-done((bf16[400,128]{1,0:T(8,128)(2,1)S(1)}, bf16[400,128]{1,0:T(8,128)(2,1)S(1)}, u32[]{:S(2)}, u32[]{:S(2)}) %collective-permute-start.12) | collective-permute-done | bytes 102432 | tf_op jit(solution)/shard_map/ppermute | solution.py:406
  69.8 1.9 %collective-permute-start.13 = (bf16[384,128]{1,0:T(8,128)(2,1)S(1)}, bf16[384,128]{1,0:T(8,128)(2,1)S(1)}, u32[]{:S(2)}, u32[]{:S(2)}) collective-permute-start(bf16[384,128]{1,0:T(8,128)(2,1)S(1)} %merge.1.refs_0_), channel_id=1, source_target_pairs={{0,1},{1,0},{2,3},{3,2},{4,5},{5,4},{6,7},{7,6},{8,9},{9,8},{10,11... | collective-permute-start | bytes 294920 | tf_op jit(solution)/shard_map/ppermute | solution.py:521
  71.7 0.9 %collective-permute-start.14 = (bf16[384,128]{1,0:T(8,128)(2,1)S(1)}, bf16[384,128]{1,0:T(8,128)(2,1)S(1)}, u32[]{:S(2)}, u32[]{:S(2)}) collective-permute-start(bf16[384,128]{1,0:T(8,128)(2,1)S(1)} %merge.1.refs_0_), channel_id=1, source_target_pairs={{0,2},{1,3},{2,0},{3,1},{4,6},{5,7},{6,4},{7,5},{8,10},{9,11},{10,... | collective-permute-start | bytes 294920 | tf_op jit(solution)/shard_map/ppermute | solution.py:521
  72.6 1.4 %collective-permute-start.15 = (bf16[384,128]{1,0:T(8,128)(2,1)S(1)}, bf16[384,128]{1,0:T(8,128)(2,1)S(1)}, u32[]{:S(2)}, u32[]{:S(2)}) collective-permute-start(bf16[384,128]{1,0:T(8,128)(2,1)S(1)} %merge.1.refs_0_), channel_id=1, source_target_pairs={{0,3},{1,2},{2,1},{3,0},{4,7},{5,6},{6,5},{7,4},{8,11},{9,10},{10,... | collective-permute-start | bytes 294920 | tf_op jit(solution)/shard_map/ppermute | solution.py:521
  74.5 2.8 %collective-permute-done.14.refs_2_ = bf16[384,128]{1,0:T(8,128)(2,1)S(1)} collective-permute-done((bf16[384,128]{1,0:T(8,128)(2,1)S(1)}, bf16[384,128]{1,0:T(8,128)(2,1)S(1)}, u32[]{:S(2)}, u32[]{:S(2)}) %collective-permute-start.14) | collective-permute-done | bytes 98336 | tf_op jit(solution)/shard_map/ppermute | solution.py:521
  77.4 1.1 %collective-permute-done.15.refs_3_ = bf16[384,128]{1,0:T(8,128)(2,1)S(1)} collective-permute-done((bf16[384,128]{1,0:T(8,128)(2,1)S(1)}, bf16[384,128]{1,0:T(8,128)(2,1)S(1)}, u32[]{:S(2)}, u32[]{:S(2)}) %collective-permute-start.15) | collective-permute-done | bytes 98336 | tf_op jit(solution)/shard_map/ppermute | solution.py:521
  78.5 1.5 %output_product.1 = bf16[384,768]{1,0:T(8,128)(2,1)} custom-call(bf16[384,128]{1,0:T(8,128)(2,1)S(1)} %merge.1.refs_0_, bf16[384,128]{1,0:T(8,128)(2,1)S(1)} %collective-permute-done.13.refs_1_, bf16[384,128]{1,0:T(8,128)(2,1)S(1)} %collective-permute-done.14.refs_2_, bf16[384,128]{1,0:T(8,128)(2,1)S(1)} %collective-permute-done.15.refs_3_, ...), custom_call_target="tpu_custom_call" | custom-call | flops 301989888 | bytes 1376256 | tf_op jit(solution)/shard_map/output_product/pallas_call | solution.py:468
  (41 shorter events, 6.4 us)
Async XLA Ops:
  0.0 17.2 %collective-permute-start = (bf16[384,3072]{1,0:T(8,128)(2,1)}, bf16[384,3072]{1,0:T(8,128)(2,1)S(1)}, u32[]{:S(2)}, u32[]{:S(2)}) collective-permute-start(bf16[384,3072]{1,0:T(8,128)(2,1)} %latents_ref.5), channel_id=1, source_target_pairs={{0,4},{4,0},{8,12},{12,8},{16,20},{20,16},{24,28},{28,24},{1,5},{5... | collective-permute-start | bytes 7077896 | tf_op jit(solution)/shard_map/ppermute | solution.py:141
  1.4 13.5 %collective-permute-start.5 = (bf16[384,256]{1,0:T(8,128)(2,1)S(1)}, bf16[384,256]{1,0:T(8,128)(2,1)S(1)}, u32[]{:S(2)}, u32[]{:S(2)}) collective-permute-start(bf16[384,256]{1,0:T(8,128)(2,1)S(1)} %slice.7.refs_0_), channel_id=1, source_target_pairs={{0,16},{4,20},{8,24},{12,28},{16,0},{20,4},{24,8},{28,12},{1,17},{... | collective-permute-start | bytes 589832 | tf_op jit(solution)/shard_map/ppermute | solution.py:139
  5.1 12.1 %collective-permute-start.7 = (bf16[384,256]{1,0:T(8,128)(2,1)S(1)}, bf16[384,256]{1,0:T(8,128)(2,1)S(1)}, u32[]{:S(2)}, u32[]{:S(2)}) collective-permute-start(bf16[384,256]{1,0:T(8,128)(2,1)S(1)} %slice.7.refs_0_), channel_id=1, source_target_pairs={{0,8},{4,12},{8,0},{12,4},{16,24},{20,28},{24,16},{28,20},{1,9},{5... | collective-permute-start | bytes 589832 | tf_op jit(solution)/shard_map/ppermute | solution.py:140
  15.0 11.5 %collective-permute-start.6 = (bf16[384,256]{1,0:T(8,128)(2,1)S(1)}, bf16[384,256]{1,0:T(8,128)(2,1)S(1)}, u32[]{:S(2)}, u32[]{:S(2)}) collective-permute-start(bf16[384,256]{1,0:T(8,128)(2,1)S(1)} %collective-permute-done.5.refs_1_), channel_id=1, source_target_pairs={{0,8},{4,12},{8,0},{12,4},{16,24},{20,28},{24,16},{28,20},{1,9},{5... | collective-permute-start | bytes 589832 | tf_op jit(solution)/shard_map/ppermute | solution.py:142
  15.6 16.1 %collective-permute-start.16 = (bf16[128,384]{1,0:T(8,128)(2,1)}, bf16[128,384]{1,0:T(8,128)(2,1)S(1)}, u32[]{:S(2)}, u32[]{:S(2)}) collective-permute-start(bf16[128,384]{1,0:T(8,128)(2,1)} %param.11), channel_id=1, source_target_pairs={{0,0},{1,8},{2,16},{3,24},{4,4},{5,12},{6,20},{7,28},{8,1},{9,9},{... | collective-permute-start | bytes 294920 | tf_op jit(solution)/shard_map/ppermute | solution.py:503
  26.5 5.2 %copy-start.3 = (bf16[128,384]{1,0:T(8,128)(2,1)S(1)}, bf16[128,384]{1,0:T(8,128)(2,1)}, u32[]{:S(2)}) copy-start(bf16[128,384]{1,0:T(8,128)(2,1)} %param.11) | copy-start | bytes 294916
  26.9 25.0 %collective-permute-start.8 = (f32[384,256]{1,0:T(8,128)S(1)}, f32[384,256]{1,0:T(8,128)S(1)}, u32[]{:S(2)}, u32[]{:S(2)}) collective-permute-start(f32[384,256]{1,0:T(8,128)S(1)} %get-tuple-element.19), channel_id=1, source_target_pairs={{0,4},{4,0},{8,12},{12,8},{16,20},{20,16},{24,28},{28,24},{1,5},{5... | collective-permute-start | bytes 1179656 | tf_op jit(solution)/shard_map/ppermute | solution.py:157
  27.9 16.3 %collective-permute-start.1 = (bf16[384,128]{1,0:T(8,128)(2,1)S(1)}, bf16[384,128]{1,0:T(8,128)(2,1)S(1)}, u32[]{:S(2)}, u32[]{:S(2)}) collective-permute-start(bf16[384,128]{1,0:T(8,128)(2,1)S(1)} %slice.6.refs_0_), channel_id=1, source_target_pairs={{0,8},{4,12},{8,16},{12,20},{16,24},{20,28},{24,0},{28,4},{1,9},{5... | collective-permute-start | bytes 294920 | tf_op jit(solution)/shard_map/ppermute | solution.py:144
  27.9 21.0 %collective-permute-start.2 = (bf16[384,128]{1,0:T(8,128)(2,1)S(1)}, bf16[384,128]{1,0:T(8,128)(2,1)S(1)}, u32[]{:S(2)}, u32[]{:S(2)}) collective-permute-start(bf16[384,128]{1,0:T(8,128)(2,1)S(1)} %slice.6.refs_0_), channel_id=1, source_target_pairs={{0,16},{4,20},{8,24},{12,28},{16,0},{20,4},{24,8},{28,12},{1,17},{... | collective-permute-start | bytes 294920 | tf_op jit(solution)/shard_map/ppermute | solution.py:144
  28.0 20.9 %collective-permute-start.3 = (bf16[384,128]{1,0:T(8,128)(2,1)S(1)}, bf16[384,128]{1,0:T(8,128)(2,1)S(1)}, u32[]{:S(2)}, u32[]{:S(2)}) collective-permute-start(bf16[384,128]{1,0:T(8,128)(2,1)S(1)} %slice.6.refs_0_), channel_id=1, source_target_pairs={{0,24},{4,28},{8,0},{12,4},{16,8},{20,12},{24,16},{28,20},{1,25},{... | collective-permute-start | bytes 294920 | tf_op jit(solution)/shard_map/ppermute | solution.py:144
  31.7 6.1 %collective-permute-start.17 = (bf16[128,384]{1,0:T(8,128)(2,1)S(1)}, bf16[128,384]{1,0:T(8,128)(2,1)S(1)}, u32[]{:S(2)}, u32[]{:S(2)}) collective-permute-start(bf16[128,384]{1,0:T(8,128)(2,1)S(1)} %copy-done.3), channel_id=1, source_target_pairs={{0,8},{1,16},{2,24},{3,0},{4,12},{5,20},{6,28},{7,4},{8,9},{9,17},... | collective-permute-start | bytes 294920 | tf_op jit(solution)/shard_map/ppermute | solution.py:503
  37.8 14.1 %collective-permute-start.18 = (bf16[128,384]{1,0:T(8,128)(2,1)S(1)}, bf16[128,384]{1,0:T(8,128)(2,1)S(1)}, u32[]{:S(2)}, u32[]{:S(2)}) collective-permute-start(bf16[128,384]{1,0:T(8,128)(2,1)S(1)} %copy-done.3), channel_id=1, source_target_pairs={{0,16},{1,24},{2,0},{3,8},{4,20},{5,28},{6,4},{7,12},{8,17},{9,25}... | collective-permute-start | bytes 294920 | tf_op jit(solution)/shard_map/ppermute | solution.py:503
  44.1 7.8 %copy-start.1 = (f32[2,128]{1,0:T(2,128)S(1)}, f32[2,128]{1,0:T(2,128)}, u32[]{:S(2)}) copy-start(f32[2,128]{1,0:T(2,128)} %refs_6_.1) | copy-start | bytes 3076
  44.2 8.7 %collective-permute-start.19 = (bf16[128,384]{1,0:T(8,128)(2,1)S(1)}, bf16[128,384]{1,0:T(8,128)(2,1)S(1)}, u32[]{:S(2)}, u32[]{:S(2)}) collective-permute-start(bf16[128,384]{1,0:T(8,128)(2,1)S(1)} %copy-done.3), channel_id=1, source_target_pairs={{0,24},{1,0},{2,8},{3,16},{4,28},{5,4},{6,12},{7,20},{8,25},{9,1},... | collective-permute-start | bytes 294920 | tf_op jit(solution)/shard_map/ppermute | solution.py:503
  49.6 13.4 %copy-start.2 = (bf16[256,256]{1,0:T(8,128)(2,1)S(1)}, bf16[256,256]{1,0:T(8,128)(2,1)}, u32[]{:S(2)}) copy-start(bf16[256,256]{1,0:T(8,128)(2,1)} %refs_5_.1) | copy-start | bytes 393220
  49.6 3.8 %collective-permute-start.4 = (f32[384,128]{1,0:T(8,128)S(1)}, f32[384,128]{1,0:T(8,128)S(1)}, u32[]{:S(2)}, u32[]{:S(2)}) collective-permute-start(f32[384,128]{1,0:T(8,128)S(1)} %get-tuple-element.15), channel_id=1, source_target_pairs={{0,4},{4,0},{8,12},{12,8},{16,20},{20,16},{24,28},{28,24},{1,5},{5... | collective-permute-start | bytes 589832 | tf_op jit(solution)/shard_map/ppermute | solution.py:168
  52.1 9.3 %collective-permute-start.10 = (bf16[384,256]{1,0:T(8,128)(2,1)S(1)}, bf16[384,256]{1,0:T(8,128)(2,1)S(1)}, u32[]{:S(2)}, u32[]{:S(2)}) collective-permute-start(bf16[384,256]{1,0:T(8,128)(2,1)S(1)} %shard_map.65.refs_1_.own_ref), channel_id=1, source_target_pairs={{4,8},{8,4},{20,24},{24,20},{0,0},{12,12},{16,16},{28,28},{5,9},{9... | collective-permute-start | bytes 589832 | tf_op jit(solution)/shard_map/ppermute | solution.py:404
  52.8 8.6 %collective-permute-start.9 = (bf16[384,256]{1,0:T(8,128)(2,1)S(1)}, bf16[384,256]{1,0:T(8,128)(2,1)S(1)}, u32[]{:S(2)}, u32[]{:S(2)}) collective-permute-start(bf16[384,256]{1,0:T(8,128)(2,1)S(1)} %shard_map.65.refs_1_.own_ref), channel_id=1, source_target_pairs={{0,4},{4,0},{8,12},{12,8},{16,20},{20,16},{24,28},{28,24},{1,5},{5... | collective-permute-start | bytes 589832 | tf_op jit(solution)/shard_map/ppermute | solution.py:403
  52.9 21.1 %collective-permute-start.20 = (bf16[512,384]{1,0:T(8,128)(2,1)S(1)}, bf16[512,384]{1,0:T(8,128)(2,1)S(1)}, u32[]{:S(2)}, u32[]{:S(2)}) collective-permute-start(bf16[512,384]{1,0:T(8,128)(2,1)S(1)} %constant_dynamic-update-slice_fusion.refs_4_), channel_id=1, source_target_pairs={{0,4},{4,0},{8,12},{12,8},{16,20},{20,16},{24,28},{28,24},{1,5},{5... | collective-permute-start | bytes 1179656 | tf_op jit(solution)/shard_map/ppermute | solution.py:519
  53.6 7.8 %collective-permute-start.11 = (bf16[384,128]{1,0:T(8,128)(2,1)S(1)}, bf16[384,128]{1,0:T(8,128)(2,1)S(1)}, u32[]{:S(2)}, u32[]{:S(2)}) collective-permute-start(bf16[384,128]{1,0:T(8,128)(2,1)S(1)} %shard_map.64.refs_0_), channel_id=1, source_target_pairs={{0,16},{4,20},{8,24},{12,28},{16,0},{20,4},{24,8},{28,12},{1,17},{... | collective-permute-start | bytes 294920 | tf_op jit(solution)/shard_map/ppermute | solution.py:402
  62.3 7.3 %collective-permute-start.12 = (bf16[400,128]{1,0:T(8,128)(2,1)S(1)}, bf16[400,128]{1,0:T(8,128)(2,1)S(1)}, u32[]{:S(2)}, u32[]{:S(2)}) collective-permute-start(bf16[400,128]{1,0:T(8,128)(2,1)S(1)} %reply.1), channel_id=1, source_target_pairs={{0,16},{4,20},{8,24},{12,28},{16,0},{20,4},{24,8},{28,12},{1,17},{... | collective-permute-start | bytes 307208 | tf_op jit(solution)/shard_map/ppermute | solution.py:406
  69.8 4.8 %collective-permute-start.13 = (bf16[384,128]{1,0:T(8,128)(2,1)S(1)}, bf16[384,128]{1,0:T(8,128)(2,1)S(1)}, u32[]{:S(2)}, u32[]{:S(2)}) collective-permute-start(bf16[384,128]{1,0:T(8,128)(2,1)S(1)} %merge.1.refs_0_), channel_id=1, source_target_pairs={{0,1},{1,0},{2,3},{3,2},{4,5},{5,4},{6,7},{7,6},{8,9},{9,8},{10,11... | collective-permute-start | bytes 294920 | tf_op jit(solution)/shard_map/ppermute | solution.py:521
  71.7 5.7 %collective-permute-start.14 = (bf16[384,128]{1,0:T(8,128)(2,1)S(1)}, bf16[384,128]{1,0:T(8,128)(2,1)S(1)}, u32[]{:S(2)}, u32[]{:S(2)}) collective-permute-start(bf16[384,128]{1,0:T(8,128)(2,1)S(1)} %merge.1.refs_0_), channel_id=1, source_target_pairs={{0,2},{1,3},{2,0},{3,1},{4,6},{5,7},{6,4},{7,5},{8,10},{9,11},{10,... | collective-permute-start | bytes 294920 | tf_op jit(solution)/shard_map/ppermute | solution.py:521
  72.6 5.9 %collective-permute-start.15 = (bf16[384,128]{1,0:T(8,128)(2,1)S(1)}, bf16[384,128]{1,0:T(8,128)(2,1)S(1)}, u32[]{:S(2)}, u32[]{:S(2)}) collective-permute-start(bf16[384,128]{1,0:T(8,128)(2,1)S(1)} %merge.1.refs_0_), channel_id=1, source_target_pairs={{0,3},{1,2},{2,1},{3,0},{4,7},{5,6},{6,5},{7,4},{8,11},{9,10},{10,... | collective-permute-start | bytes 294920 | tf_op jit(solution)/shard_map/ppermute | solution.py:521
  (1 other events, 1.7 us)
